TPU v7x, 256 devices: a whole 4x4x8 slice. The times are simulated.
256 devices in a mesh: modes: 4 (over y_hi, core), space: 64 (over x, y_lo, z).
Axes of the slice: x: 4, y: 4 (y_hi: 2, y_lo: 2; y = y_hi * 2 + y_lo), z: 8, core: 2. Of those that a mesh axis runs over, the one named last changes fastest.
Arguments:
- thermal_deviation_iterate: float32 [4, 256, 256], P(None, 'space'), may hold values from -6 to 6
- volumetric_source_term: float32 [4, 256, 256], P(None, 'space'), may hold values from -6 to 6
- node_substance_label: int32 [4, 256, 256], P(None, 'space'), may hold values from 0 to 2
- spectral_table_lookup: int32 [40], P('modes'), may hold values from 0 to 63
- propagation_velocity_table: float32 [64], replicated, may hold values from 0.7 to 1
- specific_heat_table: float32 [64], replicated, may hold values from 0.5 to 2
- collision_frequency_table: float32 [64, 3], replicated, may hold values from 0.08 to 0.4
- ordinate_inclination: float32 [30], replicated, may hold values from 0.05 to 1.52
- ordinate_longitude: float32 [30], replicated, may hold values from -3.140625 to 3.140625
Outputs:
- new_temperature: float32 [4, 256, 256], P(None, 'space', 'modes')
- heat_flux: float32 [3, 4, 256, 256], P(None, None, 'space', 'modes')
All inputs are finite; a program needn't handle non-finite values.
Results may differ from a plain program's by a relative error of at most 0.000078.
Values sent between devices are 32-bit elements; how exact they have to be, the bound alone decides.
A program may use at most 64 MiB of HBM per device.

v0:
```python
import jax
import jax.numpy as jnp
from jax import lax
from jax.sharding import PartitionSpec as P

SPECTRAL_BINS = 40
SWEEPS = 3
CHEB = 16


def extended(block, sides, width):
    for axis, dim in sides:
        count = lax.axis_size(axis)
        forward = [(i, i + 1) for i in range(count - 1)]
        backward = [(target, source) for source, target in forward]
        low = lax.ppermute(
            lax.slice_in_dim(block, block.shape[dim] - width, None, axis=dim), axis, forward
        )
        high = lax.ppermute(lax.slice_in_dim(block, 0, width, axis=dim), axis, backward)
        block = jnp.concatenate([low, block, high], axis=dim)
    return block


def directions(ordinate_inclination, ordinate_longitude):
    along_x = jnp.cos(ordinate_inclination)
    along_y = jnp.sin(ordinate_inclination) * jnp.cos(ordinate_longitude)
    along_z = jnp.sin(ordinate_inclination) * jnp.sin(ordinate_longitude)
    return (
        jnp.concatenate([along_x, -along_x]),
        jnp.concatenate([along_y, -along_y]),
        jnp.concatenate([along_z, -along_z]),
    )


def diffuse_apply(padded_values, padded_kappa):
    center = padded_values[1:-1, 1:-1, 1:-1]
    kappa_here = padded_kappa[1:-1, 1:-1, 1:-1]
    slices = [
        (slice(1, -1), slice(None, -2), slice(1, -1)),
        (slice(1, -1), slice(2, None), slice(1, -1)),
        (slice(1, -1), slice(1, -1), slice(None, -2)),
        (slice(1, -1), slice(1, -1), slice(2, None)),
        (slice(None, -2), slice(1, -1), slice(1, -1)),
        (slice(2, None), slice(1, -1), slice(1, -1)),
    ]
    total = jnp.zeros_like(center)
    for where in slices:
        total = total + 0.5 * (kappa_here + padded_kappa[where]) * (center - padded_values[where])
    return center + total


def chebyshev(forcing_vector, operator, top):
    theta = (top + 1.0) / 2.0
    delta = (top - 1.0) / 2.0
    sigma = theta / delta

    def advance(index, carry):
        correction, equation_mismatch, direction, rho = carry
        correction = correction + direction
        equation_mismatch = equation_mismatch - operator(direction)
        rho_new = 1.0 / (2.0 * sigma - rho)
        direction = rho_new * rho * direction + 2.0 * rho_new / delta * equation_mismatch
        return (correction, equation_mismatch, direction, rho_new)

    start = (jnp.zeros_like(forcing_vector), forcing_vector, forcing_vector / theta, 1.0 / sigma)
    return lax.fori_loop(0, CHEB, advance, start)[0]


def cell_rates(rates, type_masks):
    return (
        rates[:, 0, None, None, None] * type_masks[0]
        + rates[:, 1, None, None, None] * type_masks[1]
        + rates[:, 2, None, None, None] * type_masks[2]
    )[:, None]


def on_device(
    thermal_deviation_iterate,
    volumetric_source_term,
    node_substance_label,
    spectral_table_lookup,
    propagation_velocity_table,
    specific_heat_table,
    collision_frequency_table,
    ordinate_inclination,
    ordinate_longitude,
):
    pointwise_spectral_value = spectral_table_lookup.shape[0]
    tiled_extent = thermal_deviation_iterate.shape[2] // lax.axis_size("modes")
    table_rows = propagation_velocity_table.shape[0]
    onehot = (
        spectral_table_lookup[:, None] == jnp.arange(table_rows, dtype=jnp.int32)[None, :]
    ).astype(jnp.float32)
    highest = lax.Precision.HIGHEST
    velocity = jnp.dot(onehot, propagation_velocity_table, precision=highest)
    first_freq = lax.axis_index("modes") * pointwise_spectral_value
    spectral = (
        (first_freq + jnp.arange(pointwise_spectral_value, dtype=jnp.int32)).astype(jnp.float32)
        + 1.0
    ) / SPECTRAL_BINS
    specific_thermal_storage = jnp.dot(onehot, specific_heat_table, precision=highest) * spectral
    rates = jnp.dot(onehot, collision_frequency_table, precision=highest)
    part_rate = jnp.sum(specific_thermal_storage[:, None] * rates, axis=0)
    part_cond = jnp.sum(
        (specific_thermal_storage * velocity * velocity)[:, None] / (3.0 * rates), axis=0
    )
    rate_total, cond_total = lax.psum((part_rate, part_cond), "modes")
    along_x, along_y, along_z = directions(ordinate_inclination, ordinate_longitude)
    half_dir = ordinate_inclination.shape[0]
    masks = [(node_substance_label == kind).astype(jnp.float32) for kind in range(3)]
    node_collision_frequency = cell_rates(rates, masks)
    speed_x = velocity[:, None] * along_x[None, :]
    speed_y = velocity[:, None] * along_y[None, :]
    speed_z = velocity[:, None] * along_z[None, :]

    def expand(coef):
        return coef[:, :, None, None, None]

    abs_sum = jnp.abs(along_x) + jnp.abs(along_y) + jnp.abs(along_z)
    ordinate_weighted_sum = 2 * half_dir
    denom = expand(velocity[:, None] * abs_sum[None, :]) + node_collision_frequency
    equilibrium_emission = specific_thermal_storage[:, None, None, None, None] * (
        node_collision_frequency * thermal_deviation_iterate + volumetric_source_term
    )
    iteration_bundle = jnp.broadcast_to(
        specific_thermal_storage[:, None, None, None, None] * thermal_deviation_iterate,
        (pointwise_spectral_value, ordinate_weighted_sum) + thermal_deviation_iterate.shape,
    )
    forward_x = expand(jnp.maximum(speed_x, 0.0))
    backward_x = expand(jnp.maximum(-speed_x, 0.0))
    forward_y = expand(jnp.maximum(speed_y, 0.0))
    backward_y = expand(jnp.maximum(-speed_y, 0.0))
    forward_z = expand(jnp.maximum(speed_z, 0.0))
    backward_z = expand(jnp.maximum(-speed_z, 0.0))
    for sweep_index in range(SWEEPS):
        xpad = extended(iteration_bundle, (("space", 3),), 1)
        xterm = forward_x * xpad[:, :, :, :-2] + backward_x * xpad[:, :, :, 2:]
        ypad = jnp.pad(iteration_bundle, ((0, 0), (0, 0), (0, 0), (0, 0), (1, 1)))
        zpad = jnp.pad(iteration_bundle, ((0, 0), (0, 0), (1, 1), (0, 0), (0, 0)))
        yterm = forward_y * ypad[..., :-2] + backward_y * ypad[..., 2:]
        zterm = forward_z * zpad[:, :, :-2] + backward_z * zpad[:, :, 2:]
        iteration_bundle = (xterm + yterm + zterm + equilibrium_emission) / denom
    summed = jnp.sum(iteration_bundle, axis=1)
    numer = jnp.sum(node_collision_frequency[:, 0] * summed, axis=0) / ordinate_weighted_sum
    fluxes = [
        jnp.einsum("fd,fdpxy->pxy", coef, iteration_bundle, precision=highest)
        / ordinate_weighted_sum
        for coef in (speed_x, speed_y, speed_z)
    ]
    moments = jnp.stack([numer] + fluxes)
    leading_entry_index = lax.axis_index("modes") * tiled_extent
    whole_moments = lax.psum(moments, "modes")
    tile_moments = lax.dynamic_slice_in_dim(whole_moments, leading_entry_index, tiled_extent, 3)
    tile_types = lax.dynamic_slice_in_dim(
        node_substance_label, leading_entry_index, tiled_extent, 2
    )
    tiled_thermal_deviation = lax.dynamic_slice_in_dim(
        thermal_deviation_iterate, leading_entry_index, tiled_extent, 2
    )
    tile_masks = [(tile_types == kind).astype(jnp.float32) for kind in range(3)]
    conduct = cond_total / rate_total
    tile_kappa = (
        conduct[0] * tile_masks[0] + conduct[1] * tile_masks[1] + conduct[2] * tile_masks[2]
    )
    cell_total = (
        rate_total[0] * tile_masks[0]
        + rate_total[1] * tile_masks[1]
        + rate_total[2] * tile_masks[2]
    )
    hemisphere_ordinates = tile_moments[0] / cell_total
    top = 1.0 + 12.0 * jnp.max(conduct)
    forcing_vector = hemisphere_ordinates - tiled_thermal_deviation
    kappa_edges = extended(tile_kappa, (("modes", 2), ("space", 1)), 1)
    padded_kappa = jnp.pad(kappa_edges, ((1, 1), (0, 0), (0, 0)))

    def apply_tile(direction):
        edges = extended(direction, (("modes", 2), ("space", 1)), 1)
        return diffuse_apply(jnp.pad(edges, ((1, 1), (0, 0), (0, 0))), padded_kappa)

    correction = chebyshev(forcing_vector, apply_tile, top)
    return (hemisphere_ordinates + correction, tile_moments[1:4])


def solution(mesh):
    placed = (
        P(None, "space", None),
        P(None, "space", None),
        P(None, "space", None),
        P("modes"),
        P(),
        P(),
        P(),
        P(),
        P(),
    )
    return jax.shard_map(
        on_device,
        mesh=mesh,
        in_specs=placed,
        out_specs=(P(None, "space", "modes"), P(None, None, "space", "modes")),
        check_vma=False,
    )
```

profile of v0, /device:TPU:22, one launch (start us, length us, event | category | flops | bytes accessed | tf_op | source)
XLA Modules:
  0.0 737.0 jit_solution(17118505579713076804)
XLA Ops:
  16.3 6.8 collective-permute-start.5
  24.9 49.3 %collective-permute-done.4 = f32[10,60,4,1,256]{4,2,3,1,0:T(4,128)S(1)} collective-permute-done((f32[10,60,4,1,256]{4,2,3,1,0:T(4,128)S(1)}, f32[10,60,4,1,256]{4,2,3,1,0:T(4,128)S(1)}, u32[]{:S(2)}, u32[]{:S(2)}) %collective-permute-start.4) | collective-permute-done | bytes 2457632 | tf_op jit(solution)/shard_map/ppermute | solution.py:16
  77.2 6.3 broadcast_in_dim.7
  83.5 31.0 %add_divide_fusion.2 = f32[10,60,4,4,256]{4,2,3,1,0:T(4,128)} fusion(f32[10,60,4,4,256]{4,2,3,1,0:T(4,128)} %broadcast_in_dim.7, f32[10,60,4,1,256]{4,2,3,1,0:T(4,128)} %copy-done.3, f32[10,60,4,1,256]{4,2,3,1,0:T(4,128)S(1)} %collective-permute-done.4, f32[10,4,4,256]{3,1,2,0:T(4,128)S(1)} %copy.13, f32[10,60]{1,0:T(8,128)S(1)} %get-tuple-element.267, ...), kind=kLoop, calls=%fused_computation.49 | loop fusion | flops 39321600 | bytes 24920480 | tf_op jit(solution)/shard_map/div | solution.py:142
  119.7 7.4 %collective-permute-start.7 = (f32[10,60,4,1,256]{4,2,3,1,0:T(4,128)S(1)}, f32[10,60,4,1,256]{4,2,3,1,0:T(4,128)}, u32[]{:S(2)}, u32[]{:S(2)}) collective-permute-start(f32[10,60,4,1,256]{4,2,3,1,0:T(4,128)S(1)} %get-tuple-element.232), channel_id=1, source_target_pairs={{1,0},{2,1},{3,2},{4,3},{5,4},{6,5},{7,6},{8,7},{9,8},{10,9},{11,1... | collective-permute-start | bytes 7372808 | tf_op jit(solution)/shard_map/ppermute | solution.py:19
  127.1 50.6 %collective-permute-done.6 = f32[10,60,4,1,256]{4,2,3,1,0:T(4,128)S(1)} collective-permute-done((f32[10,60,4,1,256]{4,2,3,1,0:T(4,128)S(1)}, f32[10,60,4,1,256]{4,2,3,1,0:T(4,128)S(1)}, u32[]{:S(2)}, u32[]{:S(2)}) %collective-permute-start.6) | collective-permute-done | bytes 2457632 | tf_op jit(solution)/shard_map/ppermute | solution.py:16
  178.8 31.0 %add_divide_fusion.1 = f32[10,60,4,4,256]{4,2,3,1,0:T(4,128)} fusion(f32[10,60,4,4,256]{4,2,3,1,0:T(4,128)} %add_divide_fusion.2, f32[10,60,4,1,256]{4,2,3,1,0:T(4,128)} %collective-permute-done.7, f32[10,60,4,1,256]{4,2,3,1,0:T(4,128)S(1)} %collective-permute-done.6, f32[10,4,4,256]{3,1,2,0:T(4,128)S(1)} %copy.13, f32[10,60]{1,0:T(8,128)S(1)} %get-tuple-element.267, ...), kind=kLoop, calls=%fused_computation.48 | loop fusion | flops 39321600 | bytes 24920480 | tf_op jit(solution)/shard_map/div | solution.py:142
  209.8 5.6 fusion.91
  217.5 7.3 collective-permute-start.9
  224.8 47.1 %all-reduce.8 = (f32[3]{0:T(128)S(1)}, f32[3]{0:T(128)S(1)}) all-reduce(f32[3]{0:T(128)S(1)} %get-tuple-element.176, f32[3]{0:T(128)S(1)} %get-tuple-element.175), channel_id=1, replica_groups=mesh['modes'=4,'space'=64] {'modes'}, use_global_device_ids=true, to_apply=%region_4.5 | all-reduce | flops 6 | bytes 48 | tf_op jit(solution)/shard_map/psum | solution.py:107
  277.0 5.1 collective-permute-start.11
  285.5 8.7 %collective-permute-start.13 = (f32[4,1,66]{2,1,0:T(1,128)S(1)}, f32[4,1,66]{2,1,0:T(1,128)S(1)}, u32[]{:S(2)}, u32[]{:S(2)}) collective-permute-start(f32[4,1,66]{2,1,0:T(1,128)S(1)} %get-tuple-element.241), channel_id=1, source_target_pairs={{1,0},{2,1},{3,2},{4,3},{5,4},{6,5},{7,6},{8,7},{9,8},{10,9},{11,1... | collective-permute-start | bytes 3176 | tf_op jit(solution)/shard_map/ppermute | solution.py:19
  296.5 31.8 %fusion.87 = (f32[10,4,4,256]{3,1,2,0:T(4,128)S(1)}, f32[10,60,4,4,256]{4,2,3,1,0:T(4,128)}) fusion(f32[10,4,4,256]{3,1,2,0:T(4,128)S(1)} %copy.13, f32[10,60]{1,0:T(8,128)S(1)} %get-tuple-element.267, f32[10,4,4,256]{3,1,2,0:T(4,128)S(1)} %copy.12, f32[10,60]{1,0:T(8,128)S(1)} %get-tuple-element.269, f32[10,60,4,4,256]{4,2,3,1,0:T(4,128)} %add_divide_fusion.1, ...), kind=kLoop, calls=%fused_computation.194 | loop fusion | flops 41738240 | bytes 25084320 | tf_op jit(solution)/shard_map/reduce_sum | solution.py:143
  328.4 15.9 %fusion.22 = f32[1,4,4,256,1]{3,0,4,2,1:T(1,128)S(1)} fusion(f32[10,60,4,4,256]{4,2,3,1,0:T(4,128)} %get-tuple-element.216, f32[10,60,1,1,1]{1,0,2,3,4:T(8,128)S(1)} %get-tuple-element.256), kind=kOutput, calls=%fused_computation.58 | convolution fusion | flops 29491200 | bytes 9849184 | tf_op jit(solution)/shard_map/fd,fdpxy->pxy/dot_general | solution.py:146
  344.3 9.9 %fusion.20 = f32[1,4,4,256,1]{3,0,4,2,1:T(1,128)S(1)} fusion(f32[10,60,4,4,256]{4,2,3,1,0:T(4,128)S(1)} %copy-done.2, f32[10,60,1,1,1]{1,0,2,3,4:T(8,128)S(1)} %get-tuple-element.273), kind=kOutput, calls=%fused_computation.56 | convolution fusion | flops 29491200 | bytes 9849184 | tf_op jit(solution)/shard_map/fd,fdpxy->pxy/dot_general | solution.py:146
  354.2 9.7 %fusion.18 = f32[1,4,4,256,1]{3,0,4,2,1:T(1,128)S(1)} fusion(f32[10,60,4,4,256]{4,2,3,1,0:T(4,128)S(1)} %copy-done.2, f32[10,60,1,1,1]{1,0,2,3,4:T(8,128)S(1)} %get-tuple-element.270), kind=kOutput, calls=%fused_computation.54 | convolution fusion | flops 29491200 | bytes 9849184 | tf_op jit(solution)/shard_map/fd,fdpxy->pxy/dot_general | solution.py:146
  364.7 41.6 %all-reduce.11.cloned.1.call-done = f32[4,4,4,256]{3,2,1,0:T(4,128)} async-done(((f32[4,4,4,256]{3,2,1,0:T(4,128)}), f32[4,4,4,256]{3,2,1,0:T(4,128)}) %all-reduce.11.cloned.1.call-update) | async-done | bytes 65552 | tf_op jit(solution)/shard_map/psum | solution.py:152
  406.3 4.5 slice_add_fusion
  410.8 314.6 %while.19 = (s32[]{:T(128)}, f32[4,4,64]{2,1,0:T(4,128)S(1)}, f32[4,4,64]{2,1,0:T(4,128)S(1)}, f32[4,4,64]{2,1,0:T(4,128)S(1)}, f32[]{:T(128)}, /*index=5*/f32[4...) while((s32[]{:T(128)}, f32[4,4,64]{2,1,0:T(4,128)S(1)}, ...), condition=%wide.region_9.10_spmd.clone, body=%wide.region_8.9_spmd.clone.sunk | while | flops 68488 | bytes 103667 | solution.py:66
  410.9 4.9 collective-permute-start
  417.8 4.5 collective-permute-done.1
  422.4 6.1 collective-permute-start.2
  430.6 6.4 collective-permute-done.3
  441.7 4.0 collective-permute-done.1
  451.8 4.4 collective-permute-done.3
  460.9 4.0 collective-permute-done.1
  471.0 4.4 collective-permute-done.3
  480.1 4.0 collective-permute-done.1
  490.2 4.4 collective-permute-done.3
  499.3 4.0 collective-permute-done.1
  509.4 4.4 collective-permute-done.3
  518.6 4.0 collective-permute-done.1
  528.7 4.4 collective-permute-done.3
  537.8 4.0 collective-permute-done.1
  547.9 4.4 collective-permute-done.3
  557.0 4.0 collective-permute-done.1
  567.1 4.4 collective-permute-done.3
  576.2 4.0 collective-permute-done.1
  586.3 4.4 collective-permute-done.3
  595.4 4.0 collective-permute-done.1
  605.5 4.4 collective-permute-done.3
  614.6 4.0 collective-permute-done.1
  624.7 4.4 collective-permute-done.3
  643.9 4.4 collective-permute-done.3
  663.1 4.4 collective-permute-done.3
  682.3 4.4 collective-permute-done.3
  701.6 4.4 collective-permute-done.3
  720.8 4.4 collective-permute-done.3
  (257 shorter events, 219.8 us)
Async XLA Ops:
  7.2 399.2 %all-reduce.11.cloned.1.call-start = ((), (), s32[]{:S(2)}) async-start(), calls=%async_computation | async-start | bytes 131072 | tf_op jit(solution)/shard_map/psum | solution.py:152
  12.1 62.1 %collective-permute-start.4 = (f32[10,60,4,1,256]{4,2,3,1,0:T(4,128)S(1)}, f32[10,60,4,1,256]{4,2,3,1,0:T(4,128)S(1)}, u32[]{:S(2)}, u32[]{:S(2)}) collective-permute-start(f32[10,60,4,1,256]{4,2,3,1,0:T(4,128)S(1)} %broadcast_in_dim.6), channel_id=1, source_target_pairs={{0,1},{1,2},{2,3},{3,4},{4,5},{5,6},{6,7},{7,8},{8,9},{9,10},{10,1... | collective-permute-start | bytes 7372808 | tf_op jit(solution)/shard_map/ppermute | solution.py:16
  16.3 59.4 %collective-permute-start.5 = (f32[10,60,4,1,256]{4,2,3,1,0:T(4,128)S(1)}, f32[10,60,4,1,256]{4,2,3,1,0:T(4,128)S(1)}, u32[]{:S(2)}, u32[]{:S(2)}) collective-permute-start(f32[10,60,4,1,256]{4,2,3,1,0:T(4,128)S(1)} %broadcast_in_dim.8), channel_id=1, source_target_pairs={{1,0},{2,1},{3,2},{4,3},{5,4},{6,5},{7,6},{8,7},{9,8},{10,9},{11,1... | collective-permute-start | bytes 7372808 | tf_op jit(solution)/shard_map/ppermute | solution.py:19
  117.8 59.9 %collective-permute-start.6 = (f32[10,60,4,1,256]{4,2,3,1,0:T(4,128)S(1)}, f32[10,60,4,1,256]{4,2,3,1,0:T(4,128)S(1)}, u32[]{:S(2)}, u32[]{:S(2)}) collective-permute-start(f32[10,60,4,1,256]{4,2,3,1,0:T(4,128)S(1)} %get-tuple-element.231), channel_id=1, source_target_pairs={{0,1},{1,2},{2,3},{3,4},{4,5},{5,6},{6,7},{7,8},{8,9},{9,10},{10,1... | collective-permute-start | bytes 7372808 | tf_op jit(solution)/shard_map/ppermute | solution.py:16
  119.7 59.1 %collective-permute-start.7 = (f32[10,60,4,1,256]{4,2,3,1,0:T(4,128)S(1)}, f32[10,60,4,1,256]{4,2,3,1,0:T(4,128)}, u32[]{:S(2)}, u32[]{:S(2)}) collective-permute-start(f32[10,60,4,1,256]{4,2,3,1,0:T(4,128)S(1)} %get-tuple-element.232), channel_id=1, source_target_pairs={{1,0},{2,1},{3,2},{4,3},{5,4},{6,5},{7,6},{8,7},{9,8},{10,9},{11,1... | collective-permute-start | bytes 7372808 | tf_op jit(solution)/shard_map/ppermute | solution.py:19
  215.4 81.1 %collective-permute-start.8 = (f32[10,60,4,1,256]{4,2,3,1,0:T(4,128)}, f32[10,60,4,1,256]{4,2,3,1,0:T(4,128)S(1)}, u32[]{:S(2)}, u32[]{:S(2)}) collective-permute-start(f32[10,60,4,1,256]{4,2,3,1,0:T(4,128)} %get-tuple-element.229), channel_id=1, source_target_pairs={{0,1},{1,2},{2,3},{3,4},{4,5},{5,6},{6,7},{7,8},{8,9},{9,10},{10,1... | collective-permute-start | bytes 7372808 | tf_op jit(solution)/shard_map/ppermute | solution.py:16
  217.5 79.0 %collective-permute-start.9 = (f32[10,60,4,1,256]{4,2,3,1,0:T(4,128)}, f32[10,60,4,1,256]{4,2,3,1,0:T(4,128)}, u32[]{:S(2)}, u32[]{:S(2)}) collective-permute-start(f32[10,60,4,1,256]{4,2,3,1,0:T(4,128)} %get-tuple-element.230), channel_id=1, source_target_pairs={{1,0},{2,1},{3,2},{4,3},{5,4},{6,5},{7,6},{8,7},{9,8},{10,9},{11,1... | collective-permute-start | bytes 7372808 | tf_op jit(solution)/shard_map/ppermute | solution.py:19
  275.1 7.1 collective-permute-start.10
  277.0 6.5 collective-permute-start.11
  283.6 12.7 %collective-permute-start.12 = (f32[4,1,66]{2,1,0:T(1,128)S(1)}, f32[4,1,66]{2,1,0:T(1,128)S(1)}, u32[]{:S(2)}, u32[]{:S(2)}) collective-permute-start(f32[4,1,66]{2,1,0:T(1,128)S(1)} %get-tuple-element.242), channel_id=1, source_target_pairs={{0,1},{1,2},{2,3},{3,4},{4,5},{5,6},{6,7},{7,8},{8,9},{9,10},{10,1... | collective-permute-start | bytes 3176 | tf_op jit(solution)/shard_map/ppermute | solution.py:16
  285.5 10.8 %collective-permute-start.13 = (f32[4,1,66]{2,1,0:T(1,128)S(1)}, f32[4,1,66]{2,1,0:T(1,128)S(1)}, u32[]{:S(2)}, u32[]{:S(2)}) collective-permute-start(f32[4,1,66]{2,1,0:T(1,128)S(1)} %get-tuple-element.241), channel_id=1, source_target_pairs={{1,0},{2,1},{3,2},{4,3},{5,4},{6,5},{7,6},{8,7},{9,8},{10,9},{11,1... | collective-permute-start | bytes 3176 | tf_op jit(solution)/shard_map/ppermute | solution.py:19
  410.9 6.8 collective-permute-start
  415.9 6.5 collective-permute-start.1
  422.4 8.2 %collective-permute-start.2 = (f32[4,1,66]{2,1,0:T(1,128)S(1)}, f32[4,1,66]{2,1,0:T(1,128)S(1)}, u32[]{:S(2)}, u32[]{:S(2)}) collective-permute-start(f32[4,1,66]{2,1,0:T(1,128)S(1)} %get-tuple-element.376), channel_id=1, source_target_pairs={{1,0},{2,1},{3,2},{4,3},{5,4},{6,5},{7,6},{8,7},{9,8},{10,9},{11,1... | collective-permute-start | bytes 3176 | tf_op jit(solution)/shard_map/while/body/eval_jaxpr/ppermute | solution.py:19
  428.6 8.5 %collective-permute-start.3 = (f32[4,1,66]{2,1,0:T(1,128)S(1)}, f32[4,1,66]{2,1,0:T(1,128)S(1)}, u32[]{:S(2)}, u32[]{:S(2)}) collective-permute-start(f32[4,1,66]{2,1,0:T(1,128)S(1)} %get-tuple-element.377), channel_id=1, source_target_pairs={{0,1},{1,2},{2,3},{3,4},{4,5},{5,6},{6,7},{7,8},{8,9},{9,10},{10,1... | collective-permute-start | bytes 3176 | tf_op jit(solution)/shard_map/while/body/eval_jaxpr/ppermute | solution.py:16
  439.3 6.5 collective-permute-start.1
  447.8 8.5 %collective-permute-start.3 = (f32[4,1,66]{2,1,0:T(1,128)S(1)}, f32[4,1,66]{2,1,0:T(1,128)S(1)}, u32[]{:S(2)}, u32[]{:S(2)}) collective-permute-start(f32[4,1,66]{2,1,0:T(1,128)S(1)} %get-tuple-element.377), channel_id=1, source_target_pairs={{0,1},{1,2},{2,3},{3,4},{4,5},{5,6},{6,7},{7,8},{8,9},{9,10},{10,1... | collective-permute-start | bytes 3176 | tf_op jit(solution)/shard_map/while/body/eval_jaxpr/ppermute | solution.py:16
  458.5 6.5 collective-permute-start.1
  465.1 6.0 collective-permute-start.2
  467.0 8.5 %collective-permute-start.3 = (f32[4,1,66]{2,1,0:T(1,128)S(1)}, f32[4,1,66]{2,1,0:T(1,128)S(1)}, u32[]{:S(2)}, u32[]{:S(2)}) collective-permute-start(f32[4,1,66]{2,1,0:T(1,128)S(1)} %get-tuple-element.377), channel_id=1, source_target_pairs={{0,1},{1,2},{2,3},{3,4},{4,5},{5,6},{6,7},{7,8},{8,9},{9,10},{10,1... | collective-permute-start | bytes 3176 | tf_op jit(solution)/shard_map/while/body/eval_jaxpr/ppermute | solution.py:16
  477.7 6.5 collective-permute-start.1
  486.2 8.5 %collective-permute-start.3 = (f32[4,1,66]{2,1,0:T(1,128)S(1)}, f32[4,1,66]{2,1,0:T(1,128)S(1)}, u32[]{:S(2)}, u32[]{:S(2)}) collective-permute-start(f32[4,1,66]{2,1,0:T(1,128)S(1)} %get-tuple-element.377), channel_id=1, source_target_pairs={{0,1},{1,2},{2,3},{3,4},{4,5},{5,6},{6,7},{7,8},{8,9},{9,10},{10,1... | collective-permute-start | bytes 3176 | tf_op jit(solution)/shard_map/while/body/eval_jaxpr/ppermute | solution.py:16
  496.9 6.5 collective-permute-start.1
  505.4 8.5 %collective-permute-start.3 = (f32[4,1,66]{2,1,0:T(1,128)S(1)}, f32[4,1,66]{2,1,0:T(1,128)S(1)}, u32[]{:S(2)}, u32[]{:S(2)}) collective-permute-start(f32[4,1,66]{2,1,0:T(1,128)S(1)} %get-tuple-element.377), channel_id=1, source_target_pairs={{0,1},{1,2},{2,3},{3,4},{4,5},{5,6},{6,7},{7,8},{8,9},{9,10},{10,1... | collective-permute-start | bytes 3176 | tf_op jit(solution)/shard_map/while/body/eval_jaxpr/ppermute | solution.py:16
  516.1 6.5 collective-permute-start.1
  522.7 6.0 collective-permute-start.2
  524.6 8.5 %collective-permute-start.3 = (f32[4,1,66]{2,1,0:T(1,128)S(1)}, f32[4,1,66]{2,1,0:T(1,128)S(1)}, u32[]{:S(2)}, u32[]{:S(2)}) collective-permute-start(f32[4,1,66]{2,1,0:T(1,128)S(1)} %get-tuple-element.377), channel_id=1, source_target_pairs={{0,1},{1,2},{2,3},{3,4},{4,5},{5,6},{6,7},{7,8},{8,9},{9,10},{10,1... | collective-permute-start | bytes 3176 | tf_op jit(solution)/shard_map/while/body/eval_jaxpr/ppermute | solution.py:16
  535.3 6.5 collective-permute-start.1
  543.8 8.5 %collective-permute-start.3 = (f32[4,1,66]{2,1,0:T(1,128)S(1)}, f32[4,1,66]{2,1,0:T(1,128)S(1)}, u32[]{:S(2)}, u32[]{:S(2)}) collective-permute-start(f32[4,1,66]{2,1,0:T(1,128)S(1)} %get-tuple-element.377), channel_id=1, source_target_pairs={{0,1},{1,2},{2,3},{3,4},{4,5},{5,6},{6,7},{7,8},{8,9},{9,10},{10,1... | collective-permute-start | bytes 3176 | tf_op jit(solution)/shard_map/while/body/eval_jaxpr/ppermute | solution.py:16
  554.5 6.5 collective-permute-start.1
  563.0 8.5 %collective-permute-start.3 = (f32[4,1,66]{2,1,0:T(1,128)S(1)}, f32[4,1,66]{2,1,0:T(1,128)S(1)}, u32[]{:S(2)}, u32[]{:S(2)}) collective-permute-start(f32[4,1,66]{2,1,0:T(1,128)S(1)} %get-tuple-element.377), channel_id=1, source_target_pairs={{0,1},{1,2},{2,3},{3,4},{4,5},{5,6},{6,7},{7,8},{8,9},{9,10},{10,1... | collective-permute-start | bytes 3176 | tf_op jit(solution)/shard_map/while/body/eval_jaxpr/ppermute | solution.py:16
  573.8 6.5 collective-permute-start.1
  580.3 6.0 collective-permute-start.2
  582.2 8.5 %collective-permute-start.3 = (f32[4,1,66]{2,1,0:T(1,128)S(1)}, f32[4,1,66]{2,1,0:T(1,128)S(1)}, u32[]{:S(2)}, u32[]{:S(2)}) collective-permute-start(f32[4,1,66]{2,1,0:T(1,128)S(1)} %get-tuple-element.377), channel_id=1, source_target_pairs={{0,1},{1,2},{2,3},{3,4},{4,5},{5,6},{6,7},{7,8},{8,9},{9,10},{10,1... | collective-permute-start | bytes 3176 | tf_op jit(solution)/shard_map/while/body/eval_jaxpr/ppermute | solution.py:16
  593.0 6.5 collective-permute-start.1
  601.5 8.5 %collective-permute-start.3 = (f32[4,1,66]{2,1,0:T(1,128)S(1)}, f32[4,1,66]{2,1,0:T(1,128)S(1)}, u32[]{:S(2)}, u32[]{:S(2)}) collective-permute-start(f32[4,1,66]{2,1,0:T(1,128)S(1)} %get-tuple-element.377), channel_id=1, source_target_pairs={{0,1},{1,2},{2,3},{3,4},{4,5},{5,6},{6,7},{7,8},{8,9},{9,10},{10,1... | collective-permute-start | bytes 3176 | tf_op jit(solution)/shard_map/while/body/eval_jaxpr/ppermute | solution.py:16
  612.2 6.5 collective-permute-start.1
  620.7 8.5 %collective-permute-start.3 = (f32[4,1,66]{2,1,0:T(1,128)S(1)}, f32[4,1,66]{2,1,0:T(1,128)S(1)}, u32[]{:S(2)}, u32[]{:S(2)}) collective-permute-start(f32[4,1,66]{2,1,0:T(1,128)S(1)} %get-tuple-element.377), channel_id=1, source_target_pairs={{0,1},{1,2},{2,3},{3,4},{4,5},{5,6},{6,7},{7,8},{8,9},{9,10},{10,1... | collective-permute-start | bytes 3176 | tf_op jit(solution)/shard_map/while/body/eval_jaxpr/ppermute | solution.py:16
  631.4 6.5 collective-permute-start.1
  639.9 8.5 %collective-permute-start.3 = (f32[4,1,66]{2,1,0:T(1,128)S(1)}, f32[4,1,66]{2,1,0:T(1,128)S(1)}, u32[]{:S(2)}, u32[]{:S(2)}) collective-permute-start(f32[4,1,66]{2,1,0:T(1,128)S(1)} %get-tuple-element.377), channel_id=1, source_target_pairs={{0,1},{1,2},{2,3},{3,4},{4,5},{5,6},{6,7},{7,8},{8,9},{9,10},{10,1... | collective-permute-start | bytes 3176 | tf_op jit(solution)/shard_map/while/body/eval_jaxpr/ppermute | solution.py:16
  650.6 6.5 collective-permute-start.1
  659.1 8.5 %collective-permute-start.3 = (f32[4,1,66]{2,1,0:T(1,128)S(1)}, f32[4,1,66]{2,1,0:T(1,128)S(1)}, u32[]{:S(2)}, u32[]{:S(2)}) collective-permute-start(f32[4,1,66]{2,1,0:T(1,128)S(1)} %get-tuple-element.377), channel_id=1, source_target_pairs={{0,1},{1,2},{2,3},{3,4},{4,5},{5,6},{6,7},{7,8},{8,9},{9,10},{10,1... | collective-permute-start | bytes 3176 | tf_op jit(solution)/shard_map/while/body/eval_jaxpr/ppermute | solution.py:16
  669.8 6.5 collective-permute-start.1
  678.3 8.5 %collective-permute-start.3 = (f32[4,1,66]{2,1,0:T(1,128)S(1)}, f32[4,1,66]{2,1,0:T(1,128)S(1)}, u32[]{:S(2)}, u32[]{:S(2)}) collective-permute-start(f32[4,1,66]{2,1,0:T(1,128)S(1)} %get-tuple-element.377), channel_id=1, source_target_pairs={{0,1},{1,2},{2,3},{3,4},{4,5},{5,6},{6,7},{7,8},{8,9},{9,10},{10,1... | collective-permute-start | bytes 3176 | tf_op jit(solution)/shard_map/while/body/eval_jaxpr/ppermute | solution.py:16
  689.0 6.5 collective-permute-start.1
  697.5 8.5 %collective-permute-start.3 = (f32[4,1,66]{2,1,0:T(1,128)S(1)}, f32[4,1,66]{2,1,0:T(1,128)S(1)}, u32[]{:S(2)}, u32[]{:S(2)}) collective-permute-start(f32[4,1,66]{2,1,0:T(1,128)S(1)} %get-tuple-element.377), channel_id=1, source_target_pairs={{0,1},{1,2},{2,3},{3,4},{4,5},{5,6},{6,7},{7,8},{8,9},{9,10},{10,1... | collective-permute-start | bytes 3176 | tf_op jit(solution)/shard_map/while/body/eval_jaxpr/ppermute | solution.py:16
  708.2 6.5 collective-permute-start.1
  716.7 8.5 %collective-permute-start.3 = (f32[4,1,66]{2,1,0:T(1,128)S(1)}, f32[4,1,66]{2,1,0:T(1,128)S(1)}, u32[]{:S(2)}, u32[]{:S(2)}) collective-permute-start(f32[4,1,66]{2,1,0:T(1,128)S(1)} %get-tuple-element.377), channel_id=1, source_target_pairs={{0,1},{1,2},{2,3},{3,4},{4,5},{5,6},{6,7},{7,8},{8,9},{9,10},{10,1... | collective-permute-start | bytes 3176 | tf_op jit(solution)/shard_map/while/body/eval_jaxpr/ppermute | solution.py:16
  (33 other events, 667.1 us)
Sparse Core Ops, SparseCore 0:
  364.8 41.5 all-reduce.10
where the time goes:
time: 741 us; the launch traced here: 737 us
  waiting for transfers between devices  284 us (38%)
  starting transfers between devices  214 us (29%)
  other arithmetic  113 us (15%)
  blocking collectives  47.1 us (6%)
  matrix products  38.2 us (5%)
  local copies, waits for them, and re-layouts  22.2 us (3%)
  between operations  15.8 us (2%)
    ppermute x37, waiting for transfers between devices, extended(): lax.ppermute(lax.slice_in_dim(block, block.shape[dim] - width, None, axis...  238 us
    ppermute x37, starting transfers between devices, extended(): lax.ppermute(lax.slice_in_dim(block, block.shape[dim] - width, None, axis...  110 us
    ppermute x37, starting transfers between devices, extended(): lax.ppermute(lax.slice_in_dim(block, 0, width, axis=dim), axis, backward)  104 us
    div x2, other arithmetic, on_device(): iteration_bundle = (xterm + yterm + zterm + equilibrium_emission) / denom  61.9 us
    psum x1, blocking collectives, on_device(): rate_total, cond_total = lax.psum((part_rate, part_cond), 'modes')  47.1 us
    psum x1, waiting for transfers between devices, on_device(): whole_moments = lax.psum(moments, 'modes')  41.6 us
    dot_general x3, matrix products, on_device(): jnp.einsum('fd,fdpxy->pxy', coef, iteration_bundle, precision=highest)  35.5 us
    reduce_sum x1, other arithmetic, on_device(): summed = jnp.sum(iteration_bundle, axis=1)  31.8 us
  transfers between devices with their start and end apart: 75, of which 38 were waited for; matrix products, arithmetic and copies ran while one was open for 1% of the time, Pallas kernels for 0%

commit v1 on v0

v1 whole, which is shorter than its diff:
```python
import functools

import jax
import jax.numpy as jnp
from jax import lax
from jax.experimental import pallas as pl
from jax.experimental.pallas import tpu as pltpu
from jax.sharding import PartitionSpec as P

SPECTRAL_BINS = 40
ORDINATES = 60
CHEB = 16
FT = SPECTRAL_BINS // 8
REACH = 4
HALF_PI = 1.5707964
MESH = pl.DeviceIdType.MESH
OFFSETS = tuple(o for r in range(1, REACH + 1) for o in (r, -r))


def iota(shape, dim):
    return lax.broadcasted_iota(jnp.int32, shape, dim)


def permuted(x, chosen):
    rows = x.shape[0]
    first = x.astype(jnp.bfloat16)
    rest = x - first.astype(jnp.float32)
    second = rest.astype(jnp.bfloat16)
    third = (rest - second.astype(jnp.float32)).astype(jnp.bfloat16)
    stacked = jnp.concatenate([first, second, third], axis=0)
    out = jnp.dot(stacked, chosen, preferred_element_type=jnp.float32)
    return out[:rows] + (out[rows : 2 * rows] + out[2 * rows :])


def ones_where(cond):
    return jnp.where(cond, 1.0, 0.0).astype(jnp.bfloat16)


def kernel(
    n_space, n_modes,
    t_ref, s_ref, l_ref, idx_ref, vel_ref, heat_ref, rates_ref, pol_ref, azi_ref, azs_ref,
    out_t, out_f,
    h_t, h_s, h_l, look, raw, il, dirs, shifted, d_ref, src, srcp, lab, qt, cv, p_ref, g_ref, acc,
    w_int, w_num, w_flux, tables, t_win, l_send, l_recv, nq, n_send, n_recv, fq, f_send, f_recv,
    half_ref, r_send, r_recv, field, coup, cheb_c,
    hs, hr, ls, lr, ws, wr, ns, nr, fs, fr, rs, rr,
):
    m = lax.axis_index("modes")
    s = lax.axis_index("space")
    forward = m < n_modes // 2
    step = jnp.where(forward, 1, -1)

    def peer(j):
        return lax.rem(m + j, n_modes)

    def beside(o):
        return lax.rem(s + o + n_space, n_space)

    barrier = pltpu.get_barrier_semaphore()
    for j in range(1, n_modes):
        pl.semaphore_signal(barrier, inc=1, device_id=(peer(j), s), device_id_type=MESH)
    for o in OFFSETS:
        pl.semaphore_signal(barrier, inc=1, device_id=(m, beside(o)), device_id_type=MESH)

    y0 = 64 * m - 32
    natural = ones_where(iota((256, 128), 0) == iota((256, 128), 1) + y0)
    for z in range(4):
        raw[pl.ds(4 * z, 4), :] = t_ref[z]
        raw[pl.ds(16 + 4 * z, 4), :] = l_ref[z].astype(jnp.float32)
    windows = permuted(raw[0:32, :], natural)
    t_win[...] = windows[0:16]
    l_send[...] = windows[16:32]
    l_recv[REACH] = windows[16:32]
    look[0] = jnp.zeros((1, 128), jnp.int32)
    look[0, :, 0:10] = idx_ref[...]

    pl.semaphore_wait(barrier, n_modes - 1 + len(OFFSETS))

    def remote(source, target, send, recv, device):
        copy = pltpu.make_async_remote_copy(
            src_ref=source, dst_ref=target, send_sem=send, recv_sem=recv,
            device_id=device, device_id_type=MESH,
        )
        copy.start()
        return copy

    down = (m, beside(step))
    halo_copies = [
        remote(t_ref, h_t, hs.at[0], hr.at[0], down),
        remote(s_ref, h_s, hs.at[1], hr.at[1], down),
        remote(l_ref, h_l, hs.at[2], hr.at[2], down),
    ]
    look_copies = [
        remote(look.at[0], look.at[j], ls.at[j - 1], lr.at[j - 1], (peer(j), s))
        for j in range(1, n_modes)
    ]
    window_copies = [
        remote(l_send, l_recv.at[REACH - o], ws.at[i], wr.at[i], (m, beside(o)))
        for i, o in enumerate(OFFSETS)
    ]

    spot = iota((32, 128), 0) == iota((32, 128), 1)

    def column(row_ref):
        row = jnp.concatenate([row_ref[...], jnp.zeros((1, 98), jnp.float32)], axis=1)
        picked = jnp.where(spot, jnp.broadcast_to(row, (32, 128)), 0.0)
        return jnp.broadcast_to(jnp.sum(picked, axis=1, keepdims=True), (32, 128))

    polar, azimuth = column(pol_ref), column(azi_ref)
    sign = jnp.where(forward, 1.0, -1.0)
    u_x = jnp.cos(polar)
    u_y = jnp.sin(polar) * jnp.cos(azimuth)
    u_z = jnp.sin(polar) * jnp.sin(azimuth)
    y_up = jnp.where(jnp.abs(azimuth) < HALF_PI, sign, -sign)
    z_up = jnp.where(azimuth > 0.0, sign, -sign)
    dirs[0, 0:32, :] = u_x
    dirs[1, 0:32, :] = jnp.abs(u_y)
    dirs[2, 0:32, :] = jnp.abs(u_z)
    dirs[3, 0:32, :] = u_x + jnp.abs(u_y) + jnp.abs(u_z)
    dirs[4, 0:32, :] = y_up
    dirs[5, 0:32, :] = z_up
    dirs[6, 0:32, :] = sign * u_x
    dirs[7, 0:32, :] = sign * u_y
    dirs[8, 0:32, :] = sign * u_z

    y_of = 2 * (iota((256, 128), 0) & 127) + (iota((256, 128), 0) >> 7)
    lane = iota((256, 128), 1)
    for tile in range(2):
        w_int[:, tile * 128 : (tile + 1) * 128] = ones_where(iota((256, 128), 0) == 2 * lane + tile)
    for j in range(n_modes):
        w_num[:, j * 128 : (j + 1) * 128] = ones_where(y_of == lane + (64 * peer(j) - 32))
        w_flux[:, j * 128 : (j + 1) * 128] = ones_where((y_of == lane + 64 * peer(j)) & (lane < 64))

    for copy in look_copies:
        copy.wait_recv()
    freq = iota((SPECTRAL_BINS, 128), 0)
    slot = freq // 10
    spread = jnp.zeros((SPECTRAL_BINS, 128), jnp.float32)
    ordinal = jnp.zeros((SPECTRAL_BINS, 128), jnp.float32)
    for j in range(n_modes):
        row = jnp.broadcast_to(look[j].astype(jnp.float32), (SPECTRAL_BINS, 128))
        spread = jnp.where(slot == j, row, spread)
        owner = lax.rem(m + n_modes - j, n_modes)
        ordinal = jnp.where(slot == j, (10 * owner + 1).astype(jnp.float32), ordinal)
    within = freq - 10 * slot
    spectral = (ordinal + within.astype(jnp.float32)) / float(SPECTRAL_BINS)
    index = jnp.sum(
        jnp.where(iota((SPECTRAL_BINS, 128), 1) == within, spread, 0.0), axis=1, keepdims=True
    )
    chosen = iota((SPECTRAL_BINS, 64), 1).astype(jnp.float32) == index
    onehot = jnp.where(chosen, 1.0, 0.0)

    def looked_up(row):
        found = jnp.sum(onehot * row, axis=1, keepdims=True)
        return jnp.broadcast_to(found, (SPECTRAL_BINS, 128))

    velocity = looked_up(vel_ref[...])
    capacity = looked_up(heat_ref[...]) * spectral
    by_kind_of_f = [looked_up(rates_ref[k : k + 1, :]) for k in range(3)]
    kind_lane = iota((SPECTRAL_BINS, 128), 1)
    rate = jnp.where(kind_lane == 0, by_kind_of_f[0], jnp.where(kind_lane == 1, by_kind_of_f[1], by_kind_of_f[2]))
    kinds = iota((1, 128), 1)
    rate_total = jnp.sum(capacity * rate, axis=0, keepdims=True)
    cond = capacity * velocity * velocity / (3.0 * rate)
    cond_total = jnp.sum(cond, axis=0, keepdims=True)
    conduct = cond_total / rate_total
    for k in range(3):
        def splat(row):
            one = jnp.sum(jnp.where(kinds == k, row, 0.0), axis=1, keepdims=True)
            return jnp.broadcast_to(one, (1, 128))
        tables[k] = splat(rate_total)
        tables[3 + k] = splat(conduct)
    per_v = rate / velocity
    cap_v = capacity * velocity
    inv_v = 1.0 / velocity
    for f in range(FT):
        qt[f] = per_v[8 * f : 8 * f + 8]
        cv[f] = cap_v[8 * f : 8 * f + 8]

    for copy in halo_copies:
        copy.wait_recv()
    has = jnp.where(forward, s > 0, s < n_space - 1)
    for k in range(7):
        base = k + 1 if k < 3 else k - 3
        refs = (h_t, h_s, h_l) if k < 3 else (t_ref, s_ref, l_ref)

        def row_of(ref, z):
            return jnp.where(forward, ref[z, base : base + 1, :], ref[z, 3 - base : 4 - base, :])

        for z in range(4):
            t_row = row_of(refs[0], z)
            raw[4 * k + z : 4 * k + z + 1, :] = jnp.where(has, t_row, 0.0) if k < 3 else t_row
            if k > 0:
                at = 4 * (k - 1) + z
                s_row = row_of(refs[1], z)
                raw[32 + at : 33 + at, :] = jnp.where(has, s_row, 0.0) if k < 3 else s_row
                raw[56 + at : 57 + at, :] = row_of(refs[2], z).astype(jnp.float32)
    raw[28:32, :] = jnp.zeros((4, 256), jnp.float32)
    il[...] = permuted(raw[...], w_int[...])

    level = iota((24, 256), 0) & 3
    shifted[0] = il[0:24, :]
    shifted[3] = jnp.where(level == 0, 0.0, il[3:27, :])
    shifted[4] = jnp.where(level == 3, 0.0, il[5:29, :])
    tile_lane = iota((24, 128), 1)
    even, odd = il[4:28, 0:128], il[4:28, 128:256]
    shifted[1, :, 0:128] = jnp.where(tile_lane == 0, 0.0, pltpu.roll(odd, 1, 1))
    shifted[1, :, 128:256] = even
    shifted[2, :, 0:128] = odd
    shifted[2, :, 128:256] = jnp.where(tile_lane == 127, 0.0, pltpu.roll(even, 127, 1))

    for i in range(24):
        for tile in range(2):
            cols = slice(tile * 128, (tile + 1) * 128)
            kind = jnp.broadcast_to(il[56 + i : 57 + i, cols], (8, 128)).astype(jnp.int32)
            lab[i, tile] = kind
            temp = jnp.broadcast_to(il[4 + i : 5 + i, cols], (8, 128))
            heat = jnp.broadcast_to(il[32 + i : 33 + i, cols], (8, 128))
            for f in range(FT):
                q = jnp.take_along_axis(qt[f], kind, axis=1)
                value = q * temp + inv_v[8 * f : 8 * f + 8] * heat
                src[f, i, tile] = value
                if i >= 8:
                    srcp[f, i, tile] = cv[f] * value

    def clear(i, _):
        for which in range(4):
            for tile in range(2):
                acc[which, i, tile] = jnp.zeros((8, 128), jnp.float32)
        return 0

    lax.fori_loop(0, 16, clear, 0)

    lanes8 = iota((8, 128), 1)
    first = lax.rem(m, n_modes // 2) * 15

    def per_direction(j, _):
        d = first + j

        def coef(which):
            return dirs[which, pl.ds(d, 8, stride=0), :]

        def wide(row):
            return row

        def tall(row):
            return jnp.concatenate([row] * 3, axis=0)

        a_x, a_y, a_z, a_sum = coef(0), coef(1), coef(2), coef(3)
        y_pos, z_pos = coef(4) > 0.0, coef(5) > 0.0
        fy, by = jnp.where(y_pos, a_y, 0.0), jnp.where(y_pos, 0.0, a_y)
        fz, bz = jnp.where(z_pos, a_z, 0.0), jnp.where(z_pos, 0.0, a_z)
        for tile in range(2):
            cols = slice(tile * 128, (tile + 1) * 128)
            d_ref[tile, 0:24, :] = (
                tall(a_x) * shifted[0, :, cols]
                + tall(fy) * shifted[1, :, cols]
                + tall(by) * shifted[2, :, cols]
                + tall(fz) * shifted[3, :, cols]
                + tall(bz) * shifted[4, :, cols]
            )
        ahead = jnp.logical_xor(jnp.abs(azs_ref[d]) < HALF_PI, jnp.logical_not(forward))
        turn_0 = jnp.where(ahead, 1, 0)
        turn_1 = jnp.where(ahead, 0, 127)
        wide_x, wide_sum = wide(a_x), wide(a_sum)
        wide_y0 = jnp.where(lanes8 == 0, wide(by), wide(a_y))
        wide_y1 = jnp.where(lanes8 == 127, wide(fy), wide(a_y))
        wide_z, wide_fz, wide_bz = wide(a_z), wide(fz), wide(bz)
        up_mask = wide(coef(5)) > 0.0
        for i in range(16):
            for tile in range(2):
                p_ref[i, tile] = jnp.zeros((8, 128), jnp.float32)
                g_ref[i, tile] = jnp.zeros((8, 128), jnp.float32)

        def gathered(before, now, scale, source):
            c_x, c_y0, c_y1, c_z, c_fz, c_bz = scale
            out = [[None, None] for _ in range(4)]
            for z in range(4):
                turned = (
                    c_y0 * pltpu.roll(now[z][1], turn_0, 1),
                    c_y1 * pltpu.roll(now[z][0], turn_1, 1),
                )
                for tile in range(2):
                    if z == 0:
                        vertical = c_bz * now[1][tile]
                    elif z == 3:
                        vertical = c_fz * now[2][tile]
                    else:
                        vertical = c_z * jnp.where(up_mask, now[z - 1][tile], now[z + 1][tile])
                    out[z][tile] = (
                        (c_x * before[z][tile] + turned[tile]) + (vertical + source(z, tile))
                    )
            return out

        def per_block(f, _):
            weights = 1.0 / (wide_sum + qt[f])
            scale = (wide_x, wide_y0, wide_y1, wide_z, wide_fz, wide_bz)
            scaled = tuple(cv[f] * c for c in scale)
            g1_before = g2_before = None
            for k in range(6):
                rows = [4 * k + z for z in range(4)]
                inv = [[jnp.take_along_axis(weights, lab[r, t], axis=1) for t in range(2)] for r in rows]
                g1 = [
                    [
                        inv[z][t]
                        * (d_ref[t, pl.ds(rows[z], 8, stride=0), :] + src[f, rows[z], t])
                        for t in range(2)
                    ]
                    for z in range(4)
                ]
                g2 = None
                if k >= 1:
                    total = gathered(g1_before, g1, scale, lambda z, t: src[f, rows[z], t])
                    g2 = [[inv[z][t] * total[z][t] for t in range(2)] for z in range(4)]
                if k >= 2:
                    total = gathered(g2_before, g2, scaled, lambda z, t: srcp[f, rows[z], t])
                    for z in range(4):
                        i = 4 * (k - 2) + z
                        for t in range(2):
                            p_ref[i, t] += total[z][t]
                            g_ref[i, t] += inv[z][t] * total[z][t]
                g1_before, g2_before = g1, g2
            return 0

        lax.fori_loop(0, FT, per_block, 0)
        v_x, v_y, v_z = wide(coef(6)), wide(coef(7)), wide(coef(8))
        for i in range(16):
            for t in range(2):
                flow = g_ref[i, t]
                acc[0, i, t] += p_ref[i, t] - wide_sum * flow
                acc[1, i, t] += v_x * flow
                acc[2, i, t] += v_y * flow
                acc[3, i, t] += v_z * flow
        return 0

    lax.fori_loop(0, 15, per_direction, 0)

    def summed(which, target, base):
        for z in range(4):
            for t in range(2):
                found = [jnp.sum(acc[which, 4 * k + z, t], axis=0, keepdims=True) for k in range(4)]
                for x in range(4):
                    at = base + 4 * z + x
                    row = jnp.where(forward, found[x], found[3 - x])
                    target[at : at + 1, t * 128 : (t + 1) * 128] = row

    summed(0, nq, 0)
    moved = permuted(nq[...], w_num[...])
    n_recv[0] = moved[:, 0:128]
    for j in range(1, n_modes):
        n_send[j - 1] = moved[:, j * 128 : (j + 1) * 128]
    n_copies = [
        remote(n_send.at[j - 1], n_recv.at[j], ns.at[j - 1], nr.at[j - 1], (peer(j), s))
        for j in range(1, n_modes)
    ]
    for i in range(3):
        summed(1 + i, fq, 16 * i)
    moved = permuted(fq[...], w_flux[...])
    for j in range(n_modes):
        part = moved[:, j * 128 : (j + 1) * 128]
        packed = part[0:24] + pltpu.roll(part[24:48], 64, 1)
        if j == 0:
            f_recv[0] = packed
        else:
            f_send[j - 1] = packed
    f_copies = [
        remote(f_send.at[j - 1], f_recv.at[j], fs.at[j - 1], fr.at[j - 1], (peer(j), s))
        for j in range(1, n_modes)
    ]

    for copy in window_copies:
        copy.wait_recv()
    for b in range(2 * REACH + 1):
        for z in range(4):
            field[z, 4 * b : 4 * b + 4, :] = l_recv[b, 4 * z : 4 * z + 4, :]
    rows = 4 * (2 * REACH + 1)
    padded = rows + 4
    for z in range(4):
        field[z, rows:padded, :] = jnp.zeros((4, 128), jnp.float32)
    x_of = iota((padded, 128), 0) + 4 * (s - REACH)
    y_of_lane = iota((padded, 128), 1) + y0
    inside = (
        (x_of >= 0) & (x_of < 4 * n_space) & (iota((padded, 128), 0) < rows)
        & (y_of_lane >= 0) & (y_of_lane < 256)
    )

    def by_kind(label, base):
        return jnp.where(label == 0.0, tables[base], jnp.where(label == 1.0, tables[base + 1], tables[base + 2]))

    kappa = [jnp.where(inside, by_kind(field[z], 3), 0.0) for z in range(4)]

    def link(here, there):
        mean = 0.5 * (here + there)
        return jnp.where(here > 0.0, mean, 0.0), jnp.where((here > 0.0) & (there > 0.0), mean, 0.0)

    for z in range(4):
        here = kappa[z]
        none = jnp.zeros_like(here)
        around = [
            pltpu.roll(here, 1, 0), pltpu.roll(here, padded - 1, 0),
            pltpu.roll(here, 1, 1), pltpu.roll(here, 127, 1),
            kappa[z - 1] if z > 0 else none, kappa[z + 1] if z < 3 else none,
        ]
        diagonal = jnp.full_like(here, 1.0)
        for which, there in enumerate(around):
            whole, joint = link(here, there)
            diagonal = diagonal + whole
            coup[which, z] = joint
        coup[6, z] = diagonal

    top = 1.0 + 12.0 * jnp.maximum(jnp.maximum(tables[3], tables[4]), tables[5])
    theta = (top + 1.0) / 2.0
    delta = (top - 1.0) / 2.0
    sigma = theta / delta
    rho = 1.0 / sigma
    for k in range(CHEB - 1):
        rho_new = 1.0 / (2.0 * sigma - rho)
        cheb_c[k] = rho_new * rho
        cheb_c[CHEB + k] = 2.0 * rho_new / delta
        rho = rho_new

    for copy in n_copies:
        copy.wait_recv()
    numer = (n_recv[0] + n_recv[1]) + (n_recv[2] + n_recv[3])
    here = l_recv[REACH]
    half = numer / (float(ORDINATES) * by_kind(here, 0))
    mismatch = half - t_win[...]
    half_ref[...] = half
    r_send[...] = mismatch
    r_recv[REACH] = mismatch
    r_copies = [
        remote(r_send, r_recv.at[REACH - o], rs.at[i], rr.at[i], (m, beside(o)))
        for i, o in reversed(tuple(enumerate(OFFSETS)))
    ]

    for copy in f_copies:
        copy.wait_recv()
    flux = ((f_recv[0] + f_recv[1]) + (f_recv[2] + f_recv[3])) / float(ORDINATES)
    for i in range(3):
        for z in range(4):
            at = 16 * i + 4 * z
            out_f[i, z] = flux[at : at + 4, 0:64] if at < 24 else flux[at - 24 : at - 20, 64:128]

    for copy in r_copies:
        copy.wait_recv()
    for b in range(2 * REACH + 1):
        for z in range(4):
            field[z, 4 * b : 4 * b + 4, :] = r_recv[b, 4 * z : 4 * z + 4, :]
    mid = 4 * REACH
    start_r = [jnp.where(inside, field[z], 0.0) for z in range(4)]
    start_d = [r / theta for r in start_r]
    start_c = [d[mid : mid + 8] for d in start_d]

    def advance(k, carry):
        resid, direction, total = carry
        c_1, c_2 = cheb_c[k], cheb_c[CHEB + k]
        new_r, new_d, new_t = [], [], []
        for z in range(4):
            d = direction[z]
            applied = coup[6, z] * d
            applied = applied - coup[0, z] * pltpu.roll(d, 1, 0)
            applied = applied - coup[1, z] * pltpu.roll(d, padded - 1, 0)
            applied = applied - coup[2, z] * pltpu.roll(d, 1, 1)
            applied = applied - coup[3, z] * pltpu.roll(d, 127, 1)
            if z > 0:
                applied = applied - coup[4, z] * direction[z - 1]
            if z < 3:
                applied = applied - coup[5, z] * direction[z + 1]
            r = resid[z] - applied
            after = c_1 * d + c_2 * r
            new_r.append(r)
            new_d.append(after)
            new_t.append(total[z] + after[mid : mid + 8])
        return new_r, new_d, new_t

    _, _, correction = lax.fori_loop(0, CHEB - 1, advance, (start_r, start_d, start_c))
    for z in range(4):
        whole = half_ref[4 * z : 4 * z + 4, :] + correction[z][0:4]
        out_t[z] = pltpu.roll(whole, 96, 1)[:, 0:64]

    for copy in halo_copies + look_copies + window_copies + n_copies + f_copies + r_copies:
        copy.wait_send()


def solution(mesh):
    n_space, n_modes = mesh.shape["space"], mesh.shape["modes"]
    f32, i32 = jnp.float32, jnp.int32
    vmem = pl.BlockSpec(memory_space=pltpu.VMEM)
    dma = pltpu.SemaphoreType.DMA
    blocks = 2 * REACH + 1
    padded = 4 * blocks + 4

    def on_device(temp, source, label, lookup, vel, heat, rates, polar, azimuth):
        scratch = [
            pltpu.VMEM((4, 4, 256), f32), pltpu.VMEM((4, 4, 256), f32), pltpu.VMEM((4, 4, 256), i32),
            pltpu.VMEM((4, 1, 128), i32),
            pltpu.VMEM((80, 256), f32), pltpu.VMEM((80, 256), f32),
            pltpu.VMEM((9, 40, 128), f32), pltpu.VMEM((5, 24, 256), f32), pltpu.VMEM((2, 24 + 8, 128), f32),
            pltpu.VMEM((FT, 24, 2, 8, 128), f32), pltpu.VMEM((FT, 24, 2, 8, 128), f32),
            pltpu.VMEM((24, 2, 8, 128), i32),
            pltpu.VMEM((FT, 8, 128), f32), pltpu.VMEM((FT, 8, 128), f32),
            pltpu.VMEM((16, 2, 8, 128), f32), pltpu.VMEM((16, 2, 8, 128), f32),
            pltpu.VMEM((4, 16, 2, 8, 128), f32),
            pltpu.VMEM((256, 256), jnp.bfloat16),
            pltpu.VMEM((256, 128 * n_modes), jnp.bfloat16), pltpu.VMEM((256, 128 * n_modes), jnp.bfloat16),
            pltpu.VMEM((6, 1, 128), f32),
            pltpu.VMEM((16, 128), f32), pltpu.VMEM((16, 128), f32), pltpu.VMEM((blocks, 16, 128), f32),
            pltpu.VMEM((16, 256), f32), pltpu.VMEM((n_modes - 1, 16, 128), f32), pltpu.VMEM((n_modes, 16, 128), f32),
            pltpu.VMEM((48, 256), f32), pltpu.VMEM((n_modes - 1, 24, 128), f32), pltpu.VMEM((n_modes, 24, 128), f32),
            pltpu.VMEM((16, 128), f32), pltpu.VMEM((16, 128), f32), pltpu.VMEM((blocks, 16, 128), f32),
            pltpu.VMEM((4, padded, 128), f32), pltpu.VMEM((7, 4, padded, 128), f32),
            pltpu.VMEM((2 * CHEB, 1, 128), f32),
            dma((3,)), dma((3,)), dma((n_modes - 1,)), dma((n_modes - 1,)),
            dma((2 * REACH,)), dma((2 * REACH,)), dma((n_modes - 1,)), dma((n_modes - 1,)),
            dma((n_modes - 1,)), dma((n_modes - 1,)), dma((2 * REACH,)), dma((2 * REACH,)),
        ]
        call = pl.pallas_call(
            functools.partial(kernel, n_space, n_modes),
            out_shape=(
                jax.ShapeDtypeStruct((4, 4, 64), f32),
                jax.ShapeDtypeStruct((3, 4, 4, 64), f32),
            ),
            in_specs=[vmem] * 9 + [pl.BlockSpec(memory_space=pltpu.SMEM)],
            out_specs=(vmem, vmem),
            scratch_shapes=scratch,
            compiler_params=pltpu.CompilerParams(collective_id=0, has_side_effects=True),
        )
        return call(
            temp, source, label, lookup[None], vel[None], heat[None], rates.T,
            polar[None], azimuth[None], azimuth,
        )

    rows = P(None, "space", None)
    return jax.shard_map(
        on_device,
        mesh=mesh,
        in_specs=(rows, rows, rows, P("modes"), P(), P(), P(), P(), P()),
        out_specs=(P(None, "space", "modes"), P(None, None, "space", "modes")),
        check_vma=False,
    )
```

time: 741 us -> 62 us (0.08)
  the two profiles are of different devices: /device:TPU:22 before, /device:TPU:1 now
where the time goes in v1:
time: 62 us; the launch traced here: 61.8 us
  Pallas kernels  58.5 us (94%)
  local copies, waits for them, and re-layouts  2.64 us (4%)
  between operations  0.64 us (1%)
    pallas_call x1, Pallas kernels, on_device(): call(temp, source, label, lookup[None], vel[None], heat[None], rates.T, p...  58.5 us
    unnamed x2, local copies, waits for them, and re-layouts  2.64 us

profile of v1, /device:TPU:1, one launch (start us, length us, event | category | flops | bytes accessed | tf_op | source)
XLA Modules:
  0.0 61.8 jit_solution(13066597829761490851)
XLA Ops:
  0.6 58.5 %shard_map.104 = (f32[4,4,64]{2,1,0:T(4,128)}, f32[3,4,4,64]{3,2,1,0:T(4,128)}) custom-call(f32[4,4,256]{2,1,0:T(4,128)} %t_ref.1, f32[4,4,256]{2,1,0:T(4,128)} %s_ref.1, s32[4,4,256]{2,1,0:T(4,128)} %l_ref.1, s32[1,10]{1,0:T(1,128)} %bitcast.8, f32[1,64]{1,0:T(1,128)} %bitcast.9, f32[1,64]{1,0:T(1,128)} %bitcast.10, f32[3,64]{1,0:T(4,128)} %bitcast.7, ...), custom_call_target="tpu_custom_call" | custom-call | tf_op jit(solution)/shard_map/pallas_call | solution.py:528
  59.2 1.3 %copy.13 = f32[4,4,64]{2,1,0:T(4,128)} copy(f32[4,4,64]{2,1,0:T(4,128)} %get-tuple-element.4) | data formatting | bytes 8192
  60.5 1.3 %copy.14 = f32[3,4,4,64]{3,2,1,0:T(4,128)} copy(f32[3,4,4,64]{3,2,1,0:T(4,128)} %get-tuple-element.5) | data formatting | bytes 24576

commit v2 on v1

--- a/solution.py
+++ b/solution.py
@@ -32,6 +32,12 @@
     return out[:rows] + (out[rows : 2 * rows] + out[2 * rows :])
 
 
+def lookup(table, kind):
+    return jnp.take_along_axis(
+        table, kind, axis=1, mode="promise_in_bounds", wrap_negative_indices=False
+    )
+
+
 def ones_where(cond):
     return jnp.where(cond, 1.0, 0.0).astype(jnp.bfloat16)
 
@@ -40,7 +46,7 @@
     n_space, n_modes,
     t_ref, s_ref, l_ref, idx_ref, vel_ref, heat_ref, rates_ref, pol_ref, azi_ref, azs_ref,
     out_t, out_f,
-    h_t, h_s, h_l, look, raw, il, dirs, shifted, d_ref, src, srcp, lab, qt, cv, p_ref, g_ref, acc,
+    h_t, h_s, h_l, look, raw, il, dirs, shifted, d_ref, cells, lab, q_of, cv, p_ref, g_ref, acc,
     w_int, w_num, w_flux, tables, t_win, l_send, l_recv, nq, n_send, n_recv, fq, f_send, f_recv,
     half_ref, r_send, r_recv, field, coup, cheb_c,
     hs, hr, ls, lr, ws, wr, ns, nr, fs, fr, rs, rr,
@@ -73,6 +79,50 @@
     l_recv[REACH] = windows[16:32]
     look[0] = jnp.zeros((1, 128), jnp.int32)
     look[0, :, 0:10] = idx_ref[...]
+
+    spot = iota((32, 128), 0) == iota((32, 128), 1)
+
+    def column(row_ref):
+        row = jnp.concatenate([row_ref[...], jnp.zeros((1, 98), jnp.float32)], axis=1)
+        picked = jnp.where(spot, jnp.broadcast_to(row, (32, 128)), 0.0)
+        return jnp.broadcast_to(jnp.sum(picked, axis=1, keepdims=True), (32, 128))
+
+    polar, azimuth = column(pol_ref), column(azi_ref)
+    sign = jnp.where(forward, 1.0, -1.0)
+    u_x = jnp.cos(polar)
+    u_y = jnp.sin(polar) * jnp.cos(azimuth)
+    u_z = jnp.sin(polar) * jnp.sin(azimuth)
+    y_up = jnp.where(jnp.abs(azimuth) < HALF_PI, sign, -sign)
+    z_up = jnp.where(azimuth > 0.0, sign, -sign)
+    dirs[0, 0:32, :] = u_x
+    dirs[1, 0:32, :] = jnp.abs(u_y)
+    dirs[2, 0:32, :] = jnp.abs(u_z)
+    dirs[3, 0:32, :] = u_x + jnp.abs(u_y) + jnp.abs(u_z)
+    dirs[4, 0:32, :] = y_up
+    dirs[5, 0:32, :] = z_up
+    dirs[6, 0:32, :] = jnp.abs(u_y) / u_x
+    dirs[7, 0:32, :] = jnp.abs(u_z) / u_x
+    dirs[8, 0:32, :] = (u_x + jnp.abs(u_y) + jnp.abs(u_z)) / u_x
+    dirs[9, 0:32, :] = sign * u_y / u_x
+    dirs[10, 0:32, :] = sign * u_z / u_x
+
+    y_of = 2 * (iota((256, 128), 0) & 127) + (iota((256, 128), 0) >> 7)
+    lane = iota((256, 128), 1)
+    for tile in range(2):
+        w_int[:, tile * 128 : (tile + 1) * 128] = ones_where(iota((256, 128), 0) == 2 * lane + tile)
+    for j in range(n_modes):
+        w_num[:, j * 128 : (j + 1) * 128] = ones_where(y_of == lane + (64 * peer(j) - 32))
+        w_flux[:, j * 128 : (j + 1) * 128] = ones_where((y_of == lane + 64 * peer(j)) & (lane < 64))
+
+    def clear(j, _):
+        for i in range(32):
+            p_ref[j, i] = jnp.zeros((8, 128), jnp.float32)
+            g_ref[j, i] = jnp.zeros((8, 128), jnp.float32)
+        return 0
+
+    lax.fori_loop(0, 16, clear, 0)
+    for i in range(32):
+        acc[0, i] = jnp.zeros((8, 128), jnp.float32)
 
     pl.semaphore_wait(barrier, n_modes - 1 + len(OFFSETS))
 
@@ -98,38 +148,6 @@
         remote(l_send, l_recv.at[REACH - o], ws.at[i], wr.at[i], (m, beside(o)))
         for i, o in enumerate(OFFSETS)
     ]
-
-    spot = iota((32, 128), 0) == iota((32, 128), 1)
-
-    def column(row_ref):
-        row = jnp.concatenate([row_ref[...], jnp.zeros((1, 98), jnp.float32)], axis=1)
-        picked = jnp.where(spot, jnp.broadcast_to(row, (32, 128)), 0.0)
-        return jnp.broadcast_to(jnp.sum(picked, axis=1, keepdims=True), (32, 128))
-
-    polar, azimuth = column(pol_ref), column(azi_ref)
-    sign = jnp.where(forward, 1.0, -1.0)
-    u_x = jnp.cos(polar)
-    u_y = jnp.sin(polar) * jnp.cos(azimuth)
-    u_z = jnp.sin(polar) * jnp.sin(azimuth)
-    y_up = jnp.where(jnp.abs(azimuth) < HALF_PI, sign, -sign)
-    z_up = jnp.where(azimuth > 0.0, sign, -sign)
-    dirs[0, 0:32, :] = u_x
-    dirs[1, 0:32, :] = jnp.abs(u_y)
-    dirs[2, 0:32, :] = jnp.abs(u_z)
-    dirs[3, 0:32, :] = u_x + jnp.abs(u_y) + jnp.abs(u_z)
-    dirs[4, 0:32, :] = y_up
-    dirs[5, 0:32, :] = z_up
-    dirs[6, 0:32, :] = sign * u_x
-    dirs[7, 0:32, :] = sign * u_y
-    dirs[8, 0:32, :] = sign * u_z
-
-    y_of = 2 * (iota((256, 128), 0) & 127) + (iota((256, 128), 0) >> 7)
-    lane = iota((256, 128), 1)
-    for tile in range(2):
-        w_int[:, tile * 128 : (tile + 1) * 128] = ones_where(iota((256, 128), 0) == 2 * lane + tile)
-    for j in range(n_modes):
-        w_num[:, j * 128 : (j + 1) * 128] = ones_where(y_of == lane + (64 * peer(j) - 32))
-        w_flux[:, j * 128 : (j + 1) * 128] = ones_where((y_of == lane + 64 * peer(j)) & (lane < 64))
 
     for copy in look_copies:
         copy.wait_recv()
@@ -157,7 +175,7 @@
     velocity = looked_up(vel_ref[...])
     capacity = looked_up(heat_ref[...]) * spectral
     by_kind_of_f = [looked_up(rates_ref[k : k + 1, :]) for k in range(3)]
-    kind_lane = iota((SPECTRAL_BINS, 128), 1)
+    kind_lane = lax.rem(iota((SPECTRAL_BINS, 128), 1), 3)
     rate = jnp.where(kind_lane == 0, by_kind_of_f[0], jnp.where(kind_lane == 1, by_kind_of_f[1], by_kind_of_f[2]))
     kinds = iota((1, 128), 1)
     rate_total = jnp.sum(capacity * rate, axis=0, keepdims=True)
@@ -170,33 +188,63 @@
             return jnp.broadcast_to(one, (1, 128))
         tables[k] = splat(rate_total)
         tables[3 + k] = splat(conduct)
-    per_v = rate / velocity
     cap_v = capacity * velocity
     inv_v = 1.0 / velocity
     for f in range(FT):
-        qt[f] = per_v[8 * f : 8 * f + 8]
+        for kind in range(3):
+            q_of[3 * f + kind] = (by_kind_of_f[kind] / velocity)[8 * f : 8 * f + 8]
         cv[f] = cap_v[8 * f : 8 * f + 8]
+
+    def row_of(ref, base, z):
+        return jnp.where(forward, ref[z, base : base + 1, :], ref[z, 3 - base : 4 - base, :])
+
+    def fill_cells(i):
+        for tile in range(2):
+            cols = slice(tile * 128, (tile + 1) * 128)
+            at = 2 * i + tile
+            kind = jnp.broadcast_to(il[56 + i : 57 + i, cols], (8, 128)).astype(jnp.int32)
+            lab[at] = kind
+            is_0, is_1 = kind == 0, kind == 1
+            temp = jnp.broadcast_to(il[4 + i : 5 + i, cols], (8, 128))
+            heat = jnp.broadcast_to(il[32 + i : 33 + i, cols], (8, 128))
+            for f in range(FT):
+                q = jnp.where(is_0, q_of[3 * f], jnp.where(is_1, q_of[3 * f + 1], q_of[3 * f + 2]))
+                value = q * temp + inv_v[8 * f : 8 * f + 8] * heat
+                cells[f, at] = value
+                if i >= 8:
+                    cells[f, 48 + at - 16] = cv[f] * value
+
+    for k in range(4):
+        for z in range(4):
+            at = 4 * k + z
+            raw[at : at + 1, :] = row_of(t_ref, k, z)
+            raw[16 + at : 17 + at, :] = row_of(s_ref, k, z)
+            raw[32 + at : 33 + at, :] = row_of(l_ref, k, z).astype(jnp.float32)
+    turned = permuted(raw[0:48, :], w_int[...])
+    il[12:28, :] = turned[0:16]
+    il[40:56, :] = turned[16:32]
+    il[64:80, :] = turned[32:48]
+    il[28:32, :] = jnp.zeros((4, 256), jnp.float32)
+    for i in range(8, 24):
+        fill_cells(i)
 
     for copy in halo_copies:
         copy.wait_recv()
     has = jnp.where(forward, s > 0, s < n_space - 1)
-    for k in range(7):
-        base = k + 1 if k < 3 else k - 3
-        refs = (h_t, h_s, h_l) if k < 3 else (t_ref, s_ref, l_ref)
-
-        def row_of(ref, z):
-            return jnp.where(forward, ref[z, base : base + 1, :], ref[z, 3 - base : 4 - base, :])
-
+    raw[28:32, :] = jnp.zeros((4, 256), jnp.float32)
+    for k in range(3):
         for z in range(4):
-            t_row = row_of(refs[0], z)
-            raw[4 * k + z : 4 * k + z + 1, :] = jnp.where(has, t_row, 0.0) if k < 3 else t_row
+            at = 4 * k + z
+            raw[at : at + 1, :] = jnp.where(has, row_of(h_t, k + 1, z), 0.0)
             if k > 0:
-                at = 4 * (k - 1) + z
-                s_row = row_of(refs[1], z)
-                raw[32 + at : 33 + at, :] = jnp.where(has, s_row, 0.0) if k < 3 else s_row
-                raw[56 + at : 57 + at, :] = row_of(refs[2], z).astype(jnp.float32)
-    raw[28:32, :] = jnp.zeros((4, 256), jnp.float32)
-    il[...] = permuted(raw[...], w_int[...])
+                raw[8 + at : 9 + at, :] = jnp.where(has, row_of(h_s, k + 1, z), 0.0)
+                raw[16 + at : 17 + at, :] = row_of(h_l, k + 1, z).astype(jnp.float32)
+    turned = permuted(raw[0:32, :], w_int[...])
+    il[0:12, :] = turned[0:12]
+    il[32:40, :] = turned[12:20]
+    il[56:64, :] = turned[20:28]
+    for i in range(8):
+        fill_cells(i)
 
     level = iota((24, 256), 0) & 3
     shifted[0] = il[0:24, :]
@@ -209,44 +257,55 @@
     shifted[2, :, 0:128] = odd
     shifted[2, :, 128:256] = jnp.where(tile_lane == 127, 0.0, pltpu.roll(even, 127, 1))
 
-    for i in range(24):
-        for tile in range(2):
-            cols = slice(tile * 128, (tile + 1) * 128)
-            kind = jnp.broadcast_to(il[56 + i : 57 + i, cols], (8, 128)).astype(jnp.int32)
-            lab[i, tile] = kind
-            temp = jnp.broadcast_to(il[4 + i : 5 + i, cols], (8, 128))
-            heat = jnp.broadcast_to(il[32 + i : 33 + i, cols], (8, 128))
-            for f in range(FT):
-                q = jnp.take_along_axis(qt[f], kind, axis=1)
-                value = q * temp + inv_v[8 * f : 8 * f + 8] * heat
-                src[f, i, tile] = value
-                if i >= 8:
-                    srcp[f, i, tile] = cv[f] * value
-
-    def clear(i, _):
-        for which in range(4):
-            for tile in range(2):
-                acc[which, i, tile] = jnp.zeros((8, 128), jnp.float32)
-        return 0
-
-    lax.fori_loop(0, 16, clear, 0)
-
     lanes8 = iota((8, 128), 1)
     first = lax.rem(m, n_modes // 2) * 15
 
+    def look(j):
+        total = dirs[3, pl.ds(first + j, 8, stride=0), :]
+        slope = dirs[0, pl.ds(first + j, 8, stride=0), :]
+        weights = [[slope / (total + q_of[3 * f + kind]) for kind in range(3)] for f in range(FT)]
+        for at in range(48):
+            kind = lab[at]
+            is_0, is_1 = kind == 0, kind == 1
+            for f in range(FT):
+                w = weights[f]
+                cells[f, 80 + at] = jnp.where(is_0, w[0], jnp.where(is_1, w[1], w[2]))
+
+    def upwind_order(j):
+        angle = azs_ref[first + j]
+        ahead = jnp.logical_xor(jnp.abs(angle) < HALF_PI, jnp.logical_not(forward))
+        up = jnp.logical_xor(angle > 0.0, jnp.logical_not(forward))
+        levels = [jnp.where(up, z, 3 - z) for z in range(4)]
+        tiles = [jnp.where(ahead, q, 1 - q) for q in range(2)]
+        return levels, tiles, ahead
+
+    def stored_at(j):
+        levels, tiles, _ = upwind_order(j)
+        return [[2 * levels[z] + tiles[t] for t in range(2)] for z in range(4)]
+
+    def numerator(j):
+        held = jnp.where(j < 0, 15, j)
+        at = jnp.maximum(j, 0)
+        ratio = dirs[8, pl.ds(first + at, 8, stride=0), :]
+        place = stored_at(at)
+        for k in range(4):
+            for z in range(4):
+                for t in range(2):
+                    cell = 8 * k + place[z][t]
+                    acc[0, 8 * k + 2 * z + t] += p_ref[held, cell] - ratio * g_ref[held, cell]
+
     def per_direction(j, _):
         d = first + j
+        look(j)
+        numerator(j - 1)
 
         def coef(which):
             return dirs[which, pl.ds(d, 8, stride=0), :]
 
-        def wide(row):
-            return row
-
         def tall(row):
             return jnp.concatenate([row] * 3, axis=0)
 
-        a_x, a_y, a_z, a_sum = coef(0), coef(1), coef(2), coef(3)
+        a_x, a_y, a_z = coef(0), coef(1), coef(2)
         y_pos, z_pos = coef(4) > 0.0, coef(5) > 0.0
         fy, by = jnp.where(y_pos, a_y, 0.0), jnp.where(y_pos, 0.0, a_y)
         fz, bz = jnp.where(z_pos, a_z, 0.0), jnp.where(z_pos, 0.0, a_z)
@@ -259,86 +318,88 @@
                 + tall(fz) * shifted[3, :, cols]
                 + tall(bz) * shifted[4, :, cols]
             )
-        ahead = jnp.logical_xor(jnp.abs(azs_ref[d]) < HALF_PI, jnp.logical_not(forward))
-        turn_0 = jnp.where(ahead, 1, 0)
-        turn_1 = jnp.where(ahead, 0, 127)
-        wide_x, wide_sum = wide(a_x), wide(a_sum)
-        wide_y0 = jnp.where(lanes8 == 0, wide(by), wide(a_y))
-        wide_y1 = jnp.where(lanes8 == 127, wide(fy), wide(a_y))
-        wide_z, wide_fz, wide_bz = wide(a_z), wide(fz), wide(bz)
-        up_mask = wide(coef(5)) > 0.0
-        for i in range(16):
-            for tile in range(2):
-                p_ref[i, tile] = jnp.zeros((8, 128), jnp.float32)
-                g_ref[i, tile] = jnp.zeros((8, 128), jnp.float32)
+        levels, tiles, ahead = upwind_order(j)
+        turn = jnp.where(ahead, 1, 127)
+        place = [[2 * levels[z] + tiles[q] for q in range(2)] for z in range(4)]
+        r_y, r_z = coef(6), coef(7)
+        r_edge = jnp.where(lanes8 == jnp.where(ahead, 0, 127), 0.0, r_y)
 
         def gathered(before, now, scale, source):
-            c_x, c_y0, c_y1, c_z, c_fz, c_bz = scale
+            c_x, c_y, c_edge, c_z = scale
             out = [[None, None] for _ in range(4)]
             for z in range(4):
-                turned = (
-                    c_y0 * pltpu.roll(now[z][1], turn_0, 1),
-                    c_y1 * pltpu.roll(now[z][0], turn_1, 1),
-                )
-                for tile in range(2):
-                    if z == 0:
-                        vertical = c_bz * now[1][tile]
-                    elif z == 3:
-                        vertical = c_fz * now[2][tile]
-                    else:
-                        vertical = c_z * jnp.where(up_mask, now[z - 1][tile], now[z + 1][tile])
-                    out[z][tile] = (
-                        (c_x * before[z][tile] + turned[tile]) + (vertical + source(z, tile))
-                    )
+                along = (c_edge * pltpu.roll(now[z][1], turn, 1), c_y * now[z][0])
+                for q in range(2):
+                    behind = before[z][q] if c_x is None else c_x * before[z][q]
+                    total = (behind + along[q]) + source(z, q)
+                    out[z][q] = total + c_z * now[z - 1][q] if z > 0 else total
             return out
 
+        both = range(2)
+        scale = (None, r_y, r_edge, r_z)
+
         def per_block(f, _):
-            weights = 1.0 / (wide_sum + qt[f])
-            scale = (wide_x, wide_y0, wide_y1, wide_z, wide_fz, wide_bz)
-            scaled = tuple(cv[f] * c for c in scale)
-            g1_before = g2_before = None
+            scaled = (cv[f], cv[f] * r_y, cv[f] * r_edge, cv[f] * r_z)
+            h1_before = h2_before = None
             for k in range(6):
-                rows = [4 * k + z for z in range(4)]
-                inv = [[jnp.take_along_axis(weights, lab[r, t], axis=1) for t in range(2)] for r in rows]
-                g1 = [
+                inv = [[cells[f, 80 + 8 * k + place[z][q]] for q in both] for z in range(4)]
+                here = [[cells[f, 8 * k + place[z][q]] for q in both] for z in range(4)]
+                h1 = [
                     [
-                        inv[z][t]
-                        * (d_ref[t, pl.ds(rows[z], 8, stride=0), :] + src[f, rows[z], t])
-                        for t in range(2)
+                        inv[z][q]
+                        * (d_ref[tiles[q], pl.ds(4 * k + levels[z], 8, stride=0), :] + here[z][q])
+                        for q in both
                     ]
                     for z in range(4)
                 ]
-                g2 = None
+                h2 = None
                 if k >= 1:
-                    total = gathered(g1_before, g1, scale, lambda z, t: src[f, rows[z], t])
-                    g2 = [[inv[z][t] * total[z][t] for t in range(2)] for z in range(4)]
+                    total = gathered(h1_before, h1, scale, lambda z, q: here[z][q])
+                    h2 = [[inv[z][q] * total[z][q] for q in both] for z in range(4)]
                 if k >= 2:
-                    total = gathered(g2_before, g2, scaled, lambda z, t: srcp[f, rows[z], t])
+                    total = gathered(
+                        h2_before, h2, scaled, lambda z, q: cells[f, 48 + 8 * (k - 2) + place[z][q]]
+                    )
                     for z in range(4):
-                        i = 4 * (k - 2) + z
-                        for t in range(2):
-                            p_ref[i, t] += total[z][t]
-                            g_ref[i, t] += inv[z][t] * total[z][t]
-                g1_before, g2_before = g1, g2
+                        for q in both:
+                            i = 8 * (k - 2) + 2 * z + q
+                            p_ref[j, i] += total[z][q]
+                            g_ref[j, i] += inv[z][q] * total[z][q]
+                h1_before, h2_before = h1, h2
             return 0
 
         lax.fori_loop(0, FT, per_block, 0)
-        v_x, v_y, v_z = wide(coef(6)), wide(coef(7)), wide(coef(8))
-        for i in range(16):
-            for t in range(2):
-                flow = g_ref[i, t]
-                acc[0, i, t] += p_ref[i, t] - wide_sum * flow
-                acc[1, i, t] += v_x * flow
-                acc[2, i, t] += v_y * flow
-                acc[3, i, t] += v_z * flow
         return 0
 
     lax.fori_loop(0, 15, per_direction, 0)
+
+    numerator(14)
+    zero = jnp.zeros((8, 128), jnp.float32)
+
+    def fluxes():
+        for k in range(4):
+            def flux_of(j, totals):
+                v_y = dirs[9, pl.ds(first + j, 8, stride=0), :]
+                v_z = dirs[10, pl.ds(first + j, 8, stride=0), :]
+                place = stored_at(j)
+                out = []
+                for z in range(4):
+                    for t in range(2):
+                        flow = g_ref[j, 8 * k + place[z][t]]
+                        n = len(out)
+                        out += [totals[n] + flow, totals[n + 1] + v_y * flow, totals[n + 2] + v_z * flow]
+                return out
+
+            found = lax.fori_loop(0, 15, flux_of, [zero] * 24)
+            for n in range(8):
+                acc[1, 8 * k + n] = sign * found[3 * n]
+                acc[2, 8 * k + n] = found[3 * n + 1]
+                acc[3, 8 * k + n] = found[3 * n + 2]
 
     def summed(which, target, base):
         for z in range(4):
             for t in range(2):
-                found = [jnp.sum(acc[which, 4 * k + z, t], axis=0, keepdims=True) for k in range(4)]
+                found = [jnp.sum(acc[which, 8 * k + 2 * z + t], axis=0, keepdims=True) for k in range(4)]
                 for x in range(4):
                     at = base + 4 * z + x
                     row = jnp.where(forward, found[x], found[3 - x])
@@ -353,21 +414,6 @@
         remote(n_send.at[j - 1], n_recv.at[j], ns.at[j - 1], nr.at[j - 1], (peer(j), s))
         for j in range(1, n_modes)
     ]
-    for i in range(3):
-        summed(1 + i, fq, 16 * i)
-    moved = permuted(fq[...], w_flux[...])
-    for j in range(n_modes):
-        part = moved[:, j * 128 : (j + 1) * 128]
-        packed = part[0:24] + pltpu.roll(part[24:48], 64, 1)
-        if j == 0:
-            f_recv[0] = packed
-        else:
-            f_send[j - 1] = packed
-    f_copies = [
-        remote(f_send.at[j - 1], f_recv.at[j], fs.at[j - 1], fr.at[j - 1], (peer(j), s))
-        for j in range(1, n_modes)
-    ]
-
     for copy in window_copies:
         copy.wait_recv()
     for b in range(2 * REACH + 1):
@@ -433,13 +479,21 @@
         for i, o in reversed(tuple(enumerate(OFFSETS)))
     ]
 
-    for copy in f_copies:
-        copy.wait_recv()
-    flux = ((f_recv[0] + f_recv[1]) + (f_recv[2] + f_recv[3])) / float(ORDINATES)
+    fluxes()
     for i in range(3):
-        for z in range(4):
-            at = 16 * i + 4 * z
-            out_f[i, z] = flux[at : at + 4, 0:64] if at < 24 else flux[at - 24 : at - 20, 64:128]
+        summed(1 + i, fq, 16 * i)
+    moved = permuted(fq[...], w_flux[...])
+    for j in range(n_modes):
+        part = moved[:, j * 128 : (j + 1) * 128]
+        packed = part[0:24] + pltpu.roll(part[24:48], 64, 1)
+        if j == 0:
+            f_recv[0] = packed
+        else:
+            f_send[j - 1] = packed
+    f_copies = [
+        remote(f_send.at[j - 1], f_recv.at[j], fs.at[j - 1], fr.at[j - 1], (peer(j), s))
+        for j in range(1, n_modes)
+    ]
 
     for copy in r_copies:
         copy.wait_recv()
@@ -478,6 +532,14 @@
         whole = half_ref[4 * z : 4 * z + 4, :] + correction[z][0:4]
         out_t[z] = pltpu.roll(whole, 96, 1)[:, 0:64]
 
+    for copy in f_copies:
+        copy.wait_recv()
+    flux = ((f_recv[0] + f_recv[1]) + (f_recv[2] + f_recv[3])) / float(ORDINATES)
+    for i in range(3):
+        for z in range(4):
+            at = 16 * i + 4 * z
+            out_f[i, z] = flux[at : at + 4, 0:64] if at < 24 else flux[at - 24 : at - 20, 64:128]
+
     for copy in halo_copies + look_copies + window_copies + n_copies + f_copies + r_copies:
         copy.wait_send()
 
@@ -495,12 +557,11 @@
             pltpu.VMEM((4, 4, 256), f32), pltpu.VMEM((4, 4, 256), f32), pltpu.VMEM((4, 4, 256), i32),
             pltpu.VMEM((4, 1, 128), i32),
             pltpu.VMEM((80, 256), f32), pltpu.VMEM((80, 256), f32),
-            pltpu.VMEM((9, 40, 128), f32), pltpu.VMEM((5, 24, 256), f32), pltpu.VMEM((2, 24 + 8, 128), f32),
-            pltpu.VMEM((FT, 24, 2, 8, 128), f32), pltpu.VMEM((FT, 24, 2, 8, 128), f32),
-            pltpu.VMEM((24, 2, 8, 128), i32),
-            pltpu.VMEM((FT, 8, 128), f32), pltpu.VMEM((FT, 8, 128), f32),
-            pltpu.VMEM((16, 2, 8, 128), f32), pltpu.VMEM((16, 2, 8, 128), f32),
-            pltpu.VMEM((4, 16, 2, 8, 128), f32),
+            pltpu.VMEM((11, 40, 128), f32), pltpu.VMEM((5, 24, 256), f32), pltpu.VMEM((2, 24 + 8, 128), f32),
+            pltpu.VMEM((FT, 128, 8, 128), f32), pltpu.VMEM((48, 8, 128), i32),
+            pltpu.VMEM((3 * FT, 8, 128), f32), pltpu.VMEM((FT, 8, 128), f32),
+            pltpu.VMEM((16, 32, 8, 128), f32), pltpu.VMEM((16, 32, 8, 128), f32),
+            pltpu.VMEM((4, 32, 8, 128), f32),
             pltpu.VMEM((256, 256), jnp.bfloat16),
             pltpu.VMEM((256, 128 * n_modes), jnp.bfloat16), pltpu.VMEM((256, 128 * n_modes), jnp.bfloat16),
             pltpu.VMEM((6, 1, 128), f32),
@@ -517,8 +578,8 @@
         call = pl.pallas_call(
             functools.partial(kernel, n_space, n_modes),
             out_shape=(
-                jax.ShapeDtypeStruct((4, 4, 64), f32),
-                jax.ShapeDtypeStruct((3, 4, 4, 64), f32),
+                pltpu.VMEM((4, 4, 64), f32),
+                pltpu.VMEM((3, 4, 4, 64), f32),
             ),
             in_specs=[vmem] * 9 + [pl.BlockSpec(memory_space=pltpu.SMEM)],
             out_specs=(vmem, vmem),

time: 62 us -> 45.2 us (0.73)
  Pallas kernels: 58.5 us -> 43.2 us
  local copies, waits for them, and re-layouts: 2.64 us -> 1.21 us
    pallas_call x1, Pallas kernels: 58.5 us -> 43.2 us  [on_device(): call(temp, source, label, lookup[None], vel[None], heat[None], rates.T, p...]
    unnamed x2, local copies, waits for them, and re-layouts: 2.64 us -> 1.21 us
where the time goes in v2:
time: 45.2 us; the launch traced here: 45 us
  Pallas kernels  43.2 us (96%)
  local copies, waits for them, and re-layouts  1.21 us (3%)
  between operations  0.64 us (1%)
    pallas_call x1, Pallas kernels, on_device(): call(temp, source, label, lookup[None], vel[None], heat[None], rates.T, p...  43.2 us
    unnamed x2, local copies, waits for them, and re-layouts  1.21 us

profile of v2, /device:TPU:1, one launch (start us, length us, event | category | flops | bytes accessed | tf_op | source)
XLA Modules:
  0.0 45.0 jit_solution(516282354065091253)
XLA Ops:
  0.6 43.2 %shard_map.104 = (f32[4,4,64]{2,1,0:T(4,128)S(1)}, f32[3,4,4,64]{3,2,1,0:T(4,128)S(1)}) custom-call(f32[4,4,256]{2,1,0:T(4,128)} %t_ref.1, f32[4,4,256]{2,1,0:T(4,128)} %s_ref.1, s32[4,4,256]{2,1,0:T(4,128)} %l_ref.1, s32[1,10]{1,0:T(1,128)} %bitcast.8, f32[1,64]{1,0:T(1,128)} %bitcast.9, f32[1,64]{1,0:T(1,128)} %bitcast.10, f32[3,64]{1,0:T(4,128)} %bitcast.7, ...), custom_call_target="tpu_custom_call" | custom-call | tf_op jit(solution)/shard_map/pallas_call | solution.py:589
  43.8 0.6 %copy.13 = f32[4,4,64]{2,1,0:T(4,128)} copy(f32[4,4,64]{2,1,0:T(4,128)S(1)} %get-tuple-element.2) | data formatting | bytes 8192
  44.4 0.6 %copy.14 = f32[3,4,4,64]{3,2,1,0:T(4,128)} copy(f32[3,4,4,64]{3,2,1,0:T(4,128)S(1)} %get-tuple-element.3) | data formatting | bytes 24576

commit v3 on v2

--- a/solution.py
+++ b/solution.py
@@ -46,10 +46,10 @@
     n_space, n_modes,
     t_ref, s_ref, l_ref, idx_ref, vel_ref, heat_ref, rates_ref, pol_ref, azi_ref, azs_ref,
     out_t, out_f,
-    h_t, h_s, h_l, look, raw, il, dirs, shifted, d_ref, cells, lab, q_of, cv, p_ref, g_ref, acc,
+    h_t, h_s, h_l, look, raw, il, dirs, wind, d_ref, cells, lab, inv_ref, p_sum, g_sum, q_of, cv, p_ref, g_ref, acc,
     w_int, w_num, w_flux, tables, t_win, l_send, l_recv, nq, n_send, n_recv, fq, f_send, f_recv,
     half_ref, r_send, r_recv, field, coup, cheb_c,
-    hs, hr, ls, lr, ws, wr, ns, nr, fs, fr, rs, rr,
+    tokens, hs, hr, ls, lr, ws, wr, ns, nr, fs, fr, rs, rr,
 ):
     m = lax.axis_index("modes")
     s = lax.axis_index("space")
@@ -65,7 +65,7 @@
     barrier = pltpu.get_barrier_semaphore()
     for j in range(1, n_modes):
         pl.semaphore_signal(barrier, inc=1, device_id=(peer(j), s), device_id_type=MESH)
-    for o in OFFSETS:
+    for o in (1, -1):
         pl.semaphore_signal(barrier, inc=1, device_id=(m, beside(o)), device_id_type=MESH)
 
     y0 = 64 * m - 32
@@ -114,25 +114,28 @@
         w_num[:, j * 128 : (j + 1) * 128] = ones_where(y_of == lane + (64 * peer(j) - 32))
         w_flux[:, j * 128 : (j + 1) * 128] = ones_where((y_of == lane + 64 * peer(j)) & (lane < 64))
 
-    def clear(j, _):
-        for i in range(32):
-            p_ref[j, i] = jnp.zeros((8, 128), jnp.float32)
-            g_ref[j, i] = jnp.zeros((8, 128), jnp.float32)
-        return 0
-
-    lax.fori_loop(0, 16, clear, 0)
-    for i in range(32):
-        acc[0, i] = jnp.zeros((8, 128), jnp.float32)
-
-    pl.semaphore_wait(barrier, n_modes - 1 + len(OFFSETS))
-
-    def remote(source, target, send, recv, device):
-        copy = pltpu.make_async_remote_copy(
+    pl.semaphore_wait(barrier, n_modes + 1)
+
+    def described(source, target, send, recv, device):
+        return pltpu.make_async_remote_copy(
             src_ref=source, dst_ref=target, send_sem=send, recv_sem=recv,
             device_id=device, device_id_type=MESH,
         )
+
+    def remote(*of):
+        copy = described(*of)
         copy.start()
         return copy
+
+    def tell(level):
+        for side in range(2):
+            pl.semaphore_signal(
+                tokens.at[side, level], inc=1, device_id=(m, beside(1 - 2 * side)), device_id_type=MESH
+            )
+
+    def hear(level):
+        for side in range(2):
+            pl.semaphore_wait(tokens.at[side, level], 1)
 
     down = (m, beside(step))
     halo_copies = [
@@ -144,10 +147,13 @@
         remote(look.at[0], look.at[j], ls.at[j - 1], lr.at[j - 1], (peer(j), s))
         for j in range(1, n_modes)
     ]
-    window_copies = [
-        remote(l_send, l_recv.at[REACH - o], ws.at[i], wr.at[i], (m, beside(o)))
-        for i, o in enumerate(OFFSETS)
-    ]
+    tell(0)
+
+    def window_copies():
+        return [
+            described(l_send, l_recv.at[REACH - o], ws.at[i], wr.at[i], (m, beside(o)))
+            for i, o in enumerate(OFFSETS)
+        ]
 
     for copy in look_copies:
         copy.wait_recv()
@@ -199,20 +205,25 @@
         return jnp.where(forward, ref[z, base : base + 1, :], ref[z, 3 - base : 4 - base, :])
 
     def fill_cells(i):
+        k, z = i // 4, i % 4
         for tile in range(2):
             cols = slice(tile * 128, (tile + 1) * 128)
-            at = 2 * i + tile
             kind = jnp.broadcast_to(il[56 + i : 57 + i, cols], (8, 128)).astype(jnp.int32)
-            lab[at] = kind
             is_0, is_1 = kind == 0, kind == 1
             temp = jnp.broadcast_to(il[4 + i : 5 + i, cols], (8, 128))
             heat = jnp.broadcast_to(il[32 + i : 33 + i, cols], (8, 128))
+            spots = [(2 * a + b, 8 * k + 2 * abs(3 * a - z) + abs(b - tile)) for a in range(2) for b in range(2)]
+            for order, at in spots:
+                lab[order, at] = kind
             for f in range(FT):
                 q = jnp.where(is_0, q_of[3 * f], jnp.where(is_1, q_of[3 * f + 1], q_of[3 * f + 2]))
                 value = q * temp + inv_v[8 * f : 8 * f + 8] * heat
-                cells[f, at] = value
-                if i >= 8:
-                    cells[f, 48 + at - 16] = cv[f] * value
+                for order, at in spots:
+                    cells[order, f, at] = value
+                if k >= 2:
+                    value = cv[f] * value
+                    for order, at in spots:
+                        cells[order, f, 32 + at] = value
 
     for k in range(4):
         for z in range(4):
@@ -246,129 +257,139 @@
     for i in range(8):
         fill_cells(i)
 
-    level = iota((24, 256), 0) & 3
-    shifted[0] = il[0:24, :]
-    shifted[3] = jnp.where(level == 0, 0.0, il[3:27, :])
-    shifted[4] = jnp.where(level == 3, 0.0, il[5:29, :])
+    for k in range(7):
+        for z in range(4):
+            at = 4 * k + z
+            raw[at : at + 1, :] = il[4 * k + 3 - z : 4 * k + 4 - z, :]
+    level = iota((24, 128), 0) & 3
     tile_lane = iota((24, 128), 1)
-    even, odd = il[4:28, 0:128], il[4:28, 128:256]
-    shifted[1, :, 0:128] = jnp.where(tile_lane == 0, 0.0, pltpu.roll(odd, 1, 1))
-    shifted[1, :, 128:256] = even
-    shifted[2, :, 0:128] = odd
-    shifted[2, :, 128:256] = jnp.where(tile_lane == 127, 0.0, pltpu.roll(even, 127, 1))
+    for a, rows in enumerate((il, raw)):
+        for b in range(2):
+            near = [slice(0, 128), slice(128, 256)] if b == 0 else [slice(128, 256), slice(0, 128)]
+            for q in range(2):
+                wind[2 * a + b, 0, q] = rows[0:24, near[q]]
+                wind[2 * a + b, 2, q] = jnp.where(level == 0, 0.0, rows[3:27, near[q]])
+            edge, turn = (0, 1) if b == 0 else (127, 127)
+            wind[2 * a + b, 1, 0] = jnp.where(tile_lane == edge, 0.0, pltpu.roll(rows[4:28, near[1]], turn, 1))
+            wind[2 * a + b, 1, 1] = rows[4:28, near[0]]
 
     lanes8 = iota((8, 128), 1)
     first = lax.rem(m, n_modes // 2) * 15
-
-    def look(j):
-        total = dirs[3, pl.ds(first + j, 8, stride=0), :]
-        slope = dirs[0, pl.ds(first + j, 8, stride=0), :]
-        weights = [[slope / (total + q_of[3 * f + kind]) for kind in range(3)] for f in range(FT)]
-        for at in range(48):
-            kind = lab[at]
-            is_0, is_1 = kind == 0, kind == 1
-            for f in range(FT):
-                w = weights[f]
-                cells[f, 80 + at] = jnp.where(is_0, w[0], jnp.where(is_1, w[1], w[2]))
 
     def upwind_order(j):
         angle = azs_ref[first + j]
         ahead = jnp.logical_xor(jnp.abs(angle) < HALF_PI, jnp.logical_not(forward))
         up = jnp.logical_xor(angle > 0.0, jnp.logical_not(forward))
+        return up, ahead
+
+    both = range(2)
+    cell = [(z, q) for z in range(4) for q in both]
+
+    def stored_at(j):
+        up, ahead = upwind_order(j)
         levels = [jnp.where(up, z, 3 - z) for z in range(4)]
-        tiles = [jnp.where(ahead, q, 1 - q) for q in range(2)]
-        return levels, tiles, ahead
-
-    def stored_at(j):
-        levels, tiles, _ = upwind_order(j)
-        return [[2 * levels[z] + tiles[t] for t in range(2)] for z in range(4)]
+        tiles = [jnp.where(ahead, q, 1 - q) for q in both]
+        return [[2 * levels[z] + tiles[t] for t in both] for z in range(4)]
 
     def numerator(j):
+        place = stored_at(jnp.maximum(j, 0))
         held = jnp.where(j < 0, 15, j)
-        at = jnp.maximum(j, 0)
-        ratio = dirs[8, pl.ds(first + at, 8, stride=0), :]
-        place = stored_at(at)
         for k in range(4):
-            for z in range(4):
-                for t in range(2):
-                    cell = 8 * k + place[z][t]
-                    acc[0, 8 * k + 2 * z + t] += p_ref[held, cell] - ratio * g_ref[held, cell]
+            for z, t in cell:
+                acc[0, 8 * k + 2 * z + t] += p_ref[held, 8 * k + place[z][t]]
+
+    for i in range(32):
+        acc[0, i] = jnp.zeros((8, 128), jnp.float32)
+        p_ref[15, i] = jnp.zeros((8, 128), jnp.float32)
+    hear(0)
+    tell(1)
 
     def per_direction(j, _):
-        d = first + j
-        look(j)
+        @pl.when(j == 3)
+        def _():
+            hear(1)
+            tell(2)
+
+        @pl.when(j == 6)
+        def _():
+            hear(2)
+            for copy in window_copies():
+                copy.start()
+
         numerator(j - 1)
 
         def coef(which):
-            return dirs[which, pl.ds(d, 8, stride=0), :]
+            return dirs[which, pl.ds(first + j, 8, stride=0), :]
 
         def tall(row):
             return jnp.concatenate([row] * 3, axis=0)
 
-        a_x, a_y, a_z = coef(0), coef(1), coef(2)
-        y_pos, z_pos = coef(4) > 0.0, coef(5) > 0.0
-        fy, by = jnp.where(y_pos, a_y, 0.0), jnp.where(y_pos, 0.0, a_y)
-        fz, bz = jnp.where(z_pos, a_z, 0.0), jnp.where(z_pos, 0.0, a_z)
-        for tile in range(2):
-            cols = slice(tile * 128, (tile + 1) * 128)
-            d_ref[tile, 0:24, :] = (
-                tall(a_x) * shifted[0, :, cols]
-                + tall(fy) * shifted[1, :, cols]
-                + tall(by) * shifted[2, :, cols]
-                + tall(fz) * shifted[3, :, cols]
-                + tall(bz) * shifted[4, :, cols]
-            )
-        levels, tiles, ahead = upwind_order(j)
+        up, ahead = upwind_order(j)
+        order = jnp.where(up, 0, 2) + jnp.where(ahead, 0, 1)
         turn = jnp.where(ahead, 1, 127)
-        place = [[2 * levels[z] + tiles[q] for q in range(2)] for z in range(4)]
-        r_y, r_z = coef(6), coef(7)
+        a_x, a_y, a_z, a_sum = tall(coef(0)), tall(coef(1)), tall(coef(2)), coef(3)
+        for q in both:
+            d_ref[q, 0:24, :] = a_x * wind[order, 0, q] + (a_y * wind[order, 1, q] + a_z * wind[order, 2, q])
+        r_y, r_z, ratio = coef(6), coef(7), coef(8)
         r_edge = jnp.where(lanes8 == jnp.where(ahead, 0, 127), 0.0, r_y)
-
-        def gathered(before, now, scale, source):
-            c_x, c_y, c_edge, c_z = scale
-            out = [[None, None] for _ in range(4)]
-            for z in range(4):
-                along = (c_edge * pltpu.roll(now[z][1], turn, 1), c_y * now[z][0])
-                for q in range(2):
-                    behind = before[z][q] if c_x is None else c_x * before[z][q]
-                    total = (behind + along[q]) + source(z, q)
-                    out[z][q] = total + c_z * now[z - 1][q] if z > 0 else total
-            return out
-
-        both = range(2)
-        scale = (None, r_y, r_edge, r_z)
-
-        def per_block(f, _):
+        slope = coef(0)
+        weights = [[slope / (a_sum + q_of[3 * f + kind]) for kind in range(3)] for f in range(FT)]
+        for at in range(48):
+            kind = lab[order, at]
+            is_0, is_1 = kind == 0, kind == 1
+            for f in range(FT):
+                w = weights[f]
+                inv_ref[f, at] = jnp.where(is_0, w[0], jnp.where(is_1, w[1], w[2]))
+        for i in range(32):
+            p_sum[i] = jnp.zeros((8, 128), jnp.float32)
+            g_sum[i] = jnp.zeros((8, 128), jnp.float32)
+
+        def block(f, last):
             scaled = (cv[f], cv[f] * r_y, cv[f] * r_edge, cv[f] * r_z)
             h1_before = h2_before = None
+
+            def gathered(before, now, scale, source):
+                c_x, c_y, c_edge, c_z = scale
+                out = {}
+                for z in range(4):
+                    along = (c_edge * pltpu.roll(now[z, 1], turn, 1), c_y * now[z, 0])
+                    for q in both:
+                        behind = before[z, q] if c_x is None else c_x * before[z, q]
+                        total = (behind + along[q]) + source(2 * z + q)
+                        out[z, q] = total + c_z * now[z - 1, q] if z > 0 else total
+                return out
+
             for k in range(6):
-                inv = [[cells[f, 80 + 8 * k + place[z][q]] for q in both] for z in range(4)]
-                here = [[cells[f, 8 * k + place[z][q]] for q in both] for z in range(4)]
-                h1 = [
-                    [
-                        inv[z][q]
-                        * (d_ref[tiles[q], pl.ds(4 * k + levels[z], 8, stride=0), :] + here[z][q])
-                        for q in both
-                    ]
-                    for z in range(4)
-                ]
+                inv = {(z, q): inv_ref[f, 8 * k + 2 * z + q] for z, q in cell}
+                here = {(z, q): cells[order, f, 8 * k + 2 * z + q] for z, q in cell}
+                h1 = {
+                    (z, q): inv[z, q] * (d_ref[q, pl.ds(4 * k + z, 8, stride=0), :] + here[z, q])
+                    for z, q in cell
+                }
                 h2 = None
                 if k >= 1:
-                    total = gathered(h1_before, h1, scale, lambda z, q: here[z][q])
-                    h2 = [[inv[z][q] * total[z][q] for q in both] for z in range(4)]
+                    total = gathered(h1_before, h1, (None, r_y, r_edge, r_z), lambda i: here[i // 2, i % 2])
+                    h2 = {c: inv[c] * total[c] for c in cell}
                 if k >= 2:
-                    total = gathered(
-                        h2_before, h2, scaled, lambda z, q: cells[f, 48 + 8 * (k - 2) + place[z][q]]
-                    )
-                    for z in range(4):
-                        for q in both:
-                            i = 8 * (k - 2) + 2 * z + q
-                            p_ref[j, i] += total[z][q]
-                            g_ref[j, i] += inv[z][q] * total[z][q]
+                    total = gathered(h2_before, h2, scaled, lambda i: cells[order, f, 32 + 8 * k + i])
+                    for z, q in cell:
+                        i = 8 * (k - 2) + 2 * z + q
+                        p_new = p_sum[i] + total[z, q]
+                        g_new = g_sum[i] + inv[z, q] * total[z, q]
+                        if last:
+                            p_ref[j, i] = p_new - ratio * g_new
+                            g_ref[j, i] = g_new
+                        else:
+                            p_sum[i] = p_new
+                            g_sum[i] = g_new
                 h1_before, h2_before = h1, h2
+
+        def per_block(f, _):
+            block(f, False)
             return 0
 
-        lax.fori_loop(0, FT, per_block, 0)
+        lax.fori_loop(0, FT - 1, per_block, 0)
+        block(FT - 1, True)
         return 0
 
     lax.fori_loop(0, 15, per_direction, 0)
@@ -383,11 +404,10 @@
                 v_z = dirs[10, pl.ds(first + j, 8, stride=0), :]
                 place = stored_at(j)
                 out = []
-                for z in range(4):
-                    for t in range(2):
-                        flow = g_ref[j, 8 * k + place[z][t]]
-                        n = len(out)
-                        out += [totals[n] + flow, totals[n + 1] + v_y * flow, totals[n + 2] + v_z * flow]
+                for z, t in cell:
+                    flow = g_ref[j, 8 * k + place[z][t]]
+                    n = len(out)
+                    out += [totals[n] + flow, totals[n + 1] + v_y * flow, totals[n + 2] + v_z * flow]
                 return out
 
             found = lax.fori_loop(0, 15, flux_of, [zero] * 24)
@@ -414,7 +434,7 @@
         remote(n_send.at[j - 1], n_recv.at[j], ns.at[j - 1], nr.at[j - 1], (peer(j), s))
         for j in range(1, n_modes)
     ]
-    for copy in window_copies:
+    for copy in window_copies():
         copy.wait_recv()
     for b in range(2 * REACH + 1):
         for z in range(4):
@@ -540,7 +560,7 @@
             at = 16 * i + 4 * z
             out_f[i, z] = flux[at : at + 4, 0:64] if at < 24 else flux[at - 24 : at - 20, 64:128]
 
-    for copy in halo_copies + look_copies + window_copies + n_copies + f_copies + r_copies:
+    for copy in halo_copies + look_copies + window_copies() + n_copies + f_copies + r_copies:
         copy.wait_send()
 
 
@@ -557,10 +577,11 @@
             pltpu.VMEM((4, 4, 256), f32), pltpu.VMEM((4, 4, 256), f32), pltpu.VMEM((4, 4, 256), i32),
             pltpu.VMEM((4, 1, 128), i32),
             pltpu.VMEM((80, 256), f32), pltpu.VMEM((80, 256), f32),
-            pltpu.VMEM((11, 40, 128), f32), pltpu.VMEM((5, 24, 256), f32), pltpu.VMEM((2, 24 + 8, 128), f32),
-            pltpu.VMEM((FT, 128, 8, 128), f32), pltpu.VMEM((48, 8, 128), i32),
+            pltpu.VMEM((11, 40, 128), f32), pltpu.VMEM((4, 3, 2, 24, 128), f32), pltpu.VMEM((2, 24 + 8, 128), f32),
+            pltpu.VMEM((4, FT, 80, 8, 128), f32), pltpu.VMEM((4, 48, 8, 128), i32),
+            pltpu.VMEM((FT, 48, 8, 128), f32), pltpu.VMEM((32, 8, 128), f32), pltpu.VMEM((32, 8, 128), f32),
             pltpu.VMEM((3 * FT, 8, 128), f32), pltpu.VMEM((FT, 8, 128), f32),
-            pltpu.VMEM((16, 32, 8, 128), f32), pltpu.VMEM((16, 32, 8, 128), f32),
+            pltpu.VMEM((16, 32, 8, 128), f32), pltpu.VMEM((15, 32, 8, 128), f32),
             pltpu.VMEM((4, 32, 8, 128), f32),
             pltpu.VMEM((256, 256), jnp.bfloat16),
             pltpu.VMEM((256, 128 * n_modes), jnp.bfloat16), pltpu.VMEM((256, 128 * n_modes), jnp.bfloat16),
@@ -571,6 +592,7 @@
             pltpu.VMEM((16, 128), f32), pltpu.VMEM((16, 128), f32), pltpu.VMEM((blocks, 16, 128), f32),
             pltpu.VMEM((4, padded, 128), f32), pltpu.VMEM((7, 4, padded, 128), f32),
             pltpu.VMEM((2 * CHEB, 1, 128), f32),
+            pltpu.SemaphoreType.REGULAR((2, 3)),
             dma((3,)), dma((3,)), dma((n_modes - 1,)), dma((n_modes - 1,)),
             dma((2 * REACH,)), dma((2 * REACH,)), dma((n_modes - 1,)), dma((n_modes - 1,)),
             dma((n_modes - 1,)), dma((n_modes - 1,)), dma((2 * REACH,)), dma((2 * REACH,)),

time: 45.2 us -> 43.2 us (0.956)
  Pallas kernels: 43.2 us -> 41.2 us
    pallas_call x1, Pallas kernels: 43.2 us -> 41.2 us  [on_device(): call(temp, source, label, lookup[None], vel[None], heat[None], rates.T, p...]
where the time goes in v3:
time: 43.2 us; the launch traced here: 43 us
  Pallas kernels  41.2 us (95%)
  local copies, waits for them, and re-layouts  1.21 us (3%)
  between operations  0.64 us (1%)
    pallas_call x1, Pallas kernels, on_device(): call(temp, source, label, lookup[None], vel[None], heat[None], rates.T, p...  41.2 us
    unnamed x2, local copies, waits for them, and re-layouts  1.21 us

profile of v3, /device:TPU:1, one launch (start us, length us, event | category | flops | bytes accessed | tf_op | source)
XLA Modules:
  0.0 43.0 jit_solution(5879044332550828401)
XLA Ops:
  0.6 41.2 %shard_map.104 = (f32[4,4,64]{2,1,0:T(4,128)S(1)}, f32[3,4,4,64]{3,2,1,0:T(4,128)S(1)}) custom-call(f32[4,4,256]{2,1,0:T(4,128)} %t_ref.1, f32[4,4,256]{2,1,0:T(4,128)} %s_ref.1, s32[4,4,256]{2,1,0:T(4,128)} %l_ref.1, s32[1,10]{1,0:T(1,128)} %bitcast.8, f32[1,64]{1,0:T(1,128)} %bitcast.9, f32[1,64]{1,0:T(1,128)} %bitcast.10, f32[3,64]{1,0:T(4,128)} %bitcast.7, ...), custom_call_target="tpu_custom_call" | custom-call | tf_op jit(solution)/shard_map/pallas_call | solution.py:611
  41.8 0.6 %copy.13 = f32[4,4,64]{2,1,0:T(4,128)} copy(f32[4,4,64]{2,1,0:T(4,128)S(1)} %get-tuple-element.2) | data formatting | bytes 8192
  42.4 0.6 %copy.14 = f32[3,4,4,64]{3,2,1,0:T(4,128)} copy(f32[3,4,4,64]{3,2,1,0:T(4,128)S(1)} %get-tuple-element.3) | data formatting | bytes 24576
